TPU v7x, 32 devices: a whole 2x2x4 slice. The times are simulated.
32 devices in a mesh: section: 2 (over core), blk: 8 (over z, y), head: 2 (over x).
Axes of the slice: x: 2, y: 2, z: 4, core: 2. Of those that a mesh axis runs over, the one named last changes fastest.
Arguments:
- projected: bfloat16 [8192, 8192], P(('section', 'blk')), may hold values from -6 to 6
- key_weight: bfloat16 [8192, 1024], P(None, 'head'), may hold values from -0.0625 to 0.0625
- value_weight: bfloat16 [8192, 1024], P(None, 'head'), may hold values from -0.0625 to 0.0625
- key_gain: float32 [128], replicated, may hold values from 0.1 to 1.9
- queries: bfloat16 [1024, 8, 1024], P('blk', 'section', 'head'), may hold values from -320 to 320
- frame_tokens: int32 [32], replicated, may hold values from 1 to 512, 8192 in all
- span_first: int32 [1024], replicated, may hold values from 0 to 31
- span_count: int32 [1024], replicated, may hold values from 1 to 32
Outputs:
- attended: bfloat16 [1024, 8, 1024], P('blk', 'section', 'head')
Inputs may be any that keep to these rules, and one draw needn't show every extreme that they name: Frame f holds frame_tokens[f] consecutive visual tokens, and they sum to 8192.
All inputs are finite; a program needn't handle non-finite values.
Results may differ from a plain program's by a relative error of at most 0.005.
The roundings to bfloat16 on the way count: a program that leaves them out, or rounds other values in their place, can miss the bound.
Values may be sent and summed in bfloat16 or wider, within the bound.
No kernel may reach another device: no remote copies, remote signals or barrier semaphores. Data moves between devices by JAX's collectives and lax.ppermute only.
A program may use at most 192 MiB of HBM per device.

v0:
```python
import jax
import jax.numpy as jnp
from jax import lax
from jax.sharding import PartitionSpec as P

HD = 128
FRAMES = 32


def span_bounds(frame_tokens, span_first, span_count):
    frame_ids = jnp.arange(FRAMES, dtype=jnp.int32)
    span_end = jnp.minimum(span_first + span_count, FRAMES)
    first_token = jnp.sum(
        jnp.where(frame_ids[None, :] < span_first[:, None], frame_tokens[None, :], 0), axis=1
    )
    end_token = jnp.sum(
        jnp.where(frame_ids[None, :] < span_end[:, None], frame_tokens[None, :], 0), axis=1
    )
    return (first_token, end_token)


def make_tables(projected, key_weight, value_weight, key_gain):
    count_rows = projected.shape[0]
    local_heads = key_weight.shape[1] // HD
    key_raw = jnp.dot(projected, key_weight, preferred_element_type=jnp.float32).reshape(
        count_rows, local_heads, HD
    )
    mean_square = jnp.mean(key_raw * key_raw, axis=2, keepdims=True)
    key_block = (key_raw / jnp.sqrt(mean_square + 1e-05) * key_gain).astype(jnp.bfloat16)
    value_block = (
        jnp.dot(projected, value_weight, preferred_element_type=jnp.float32)
        .astype(jnp.bfloat16)
        .reshape(count_rows, local_heads, HD)
    )
    return (key_block, value_block)


def masked_scores(query_block, key_block, key_positions, first_token, end_token):
    scores = jnp.einsum(
        "npgd,mgd->gnpm", query_block, key_block, preferred_element_type=jnp.float32
    ) * HD ** (-0.5)
    allowed = (key_positions[None, :] >= first_token[:, None]) & (
        key_positions[None, :] < end_token[:, None]
    )
    return jnp.where(allowed[None, :, None, :], scores, -1e30)


def weighted_sum(scores, row_max, value_block):
    weights = jnp.exp(scores - row_max[..., None])
    denominator = jnp.sum(weights, axis=3)
    numerator = jnp.einsum(
        "gnpm,mgd->npgd",
        weights.astype(jnp.bfloat16),
        value_block,
        preferred_element_type=jnp.float32,
    )
    return (numerator, jnp.transpose(denominator, (1, 2, 0)))


def body(
    projected, key_weight, value_weight, key_gain, queries, frame_tokens, span_first, span_count
):
    key_block, value_block = make_tables(projected, key_weight, value_weight, key_gain)
    first_token, end_token = span_bounds(frame_tokens, span_first, span_count)
    own_rows = queries.shape[0]
    sub_heads = queries.shape[1]
    local_heads = key_block.shape[1]
    count_rows = key_block.shape[0]
    section_count = lax.axis_size("section")
    block_count = lax.axis_size("blk")
    block_index = lax.axis_index("blk")
    section_ids = jnp.arange(section_count, dtype=jnp.int32)
    row_ids = jnp.arange(count_rows, dtype=jnp.int32)
    pair_keys, pair_values = (
        lax.all_gather(key_block, "section", axis=0, tiled=True),
        lax.all_gather(value_block, "section", axis=0, tiled=True),
    )
    all_keys, all_values = (
        lax.all_gather(pair_keys, "blk", axis=0, tiled=True),
        lax.all_gather(pair_values, "blk", axis=0, tiled=True),
    )
    block_ids = jnp.arange(block_count, dtype=jnp.int32)
    key_positions = (
        (section_ids[None, :, None] * block_count + block_ids[:, None, None]) * count_rows
        + row_ids[None, None, :]
    ).reshape(-1)
    own_first = lax.dynamic_slice_in_dim(first_token, block_index * own_rows, own_rows)
    own_end = lax.dynamic_slice_in_dim(end_token, block_index * own_rows, own_rows)
    shaped = queries.reshape(own_rows, sub_heads, local_heads, HD)
    scores = masked_scores(shaped, all_keys, key_positions, own_first, own_end)
    row_max = jnp.max(scores, axis=3)
    numerator, denominator = weighted_sum(scores, row_max, all_values)
    attended = numerator / denominator[..., None]
    return attended.astype(jnp.bfloat16).reshape(own_rows, sub_heads, local_heads * HD)


def solution(mesh):
    placed = (
        P(("section", "blk"), None),
        P(None, "head"),
        P(None, "head"),
        P(),
        P("blk", "section", "head"),
        P(),
        P(),
        P(),
    )
    return jax.shard_map(
        body, mesh=mesh, in_specs=placed, out_specs=P("blk", "section", "head"), check_vma=False
    )
```

profile of v0, /device:TPU:0, one launch (start us, length us, event | category | flops | bytes accessed | tf_op | source)
XLA Modules:
  0.0 328.6 jit_solution(8229665058144376835)
XLA Ops:
  6.5 9.5 %multiply_reduce_fusion = (f32[512,4]{0,1:T(4,128)S(1)}, f32[512,512]{0,1:T(8,128)S(1)}) fusion(bf16[512,8192]{1,0:T(8,128)(2,1)} %param.8, bf16[8192,512]{1,0:T(8,128)(2,1)} %param.9), kind=kOutput, calls=%fused_computation.16 | convolution fusion | flops 4295489536 | bytes 17833984 | tf_op jit(solution)/shard_map/dot_general | solution.py:25
  16.0 0.3 copy.17
  16.4 1.1 multiply_convert_fusion
  17.5 0.0 all-gather.9.cloned.1.call-update
  17.6 0.0 all-gather.5.cloned.1.call-start
  17.6 11.2 %convolution_convert_fusion = bf16[512,512]{0,1:T(8,128)(2,1)} fusion(bf16[512,8192]{1,0:T(8,128)(2,1)} %param.8, bf16[8192,512]{1,0:T(8,128)(2,1)} %param.10), kind=kOutput, calls=%fused_computation.12 | convolution fusion | flops 4295229440 | bytes 17301504 | tf_op jit(solution)/shard_map/dot_general | solution.py:31
  28.8 0.0 all-gather.5.cloned.1.call-update
  28.8 0.0 all-gather.11.cloned.1.call-start
  28.9 0.6 all-gather.9.cloned.1.call-done
  29.5 0.1 all-gather.11.cloned.1.call-update
  29.6 0.2 all-gather.7.cloned.1.call-start
  29.8 11.4 %all-gather.5.cloned.1.call-done = bf16[1024,4,128]{0,2,1:T(8,128)(2,1)} async-done(((bf16[512,4,128]{0,2,1:T(8,128)(2,1)}), bf16[1024,4,128]{0,2,1:T(8,128)(2,1)}) %all-gather.5.cloned.1.call-update) | async-done | bytes 1048592 | tf_op jit(solution)/shard_map/all_gather | solution.py:76
  41.3 0.1 select_reduce_fusion.1
  41.4 0.1 dynamic_slice.7
  41.5 0.1 dynamic_slice.6
  41.6 0.1 add_bitcast_fusion
  41.7 0.2 reshape.125
  41.9 3.7 %compare_and_fusion = pred[128,8192]{0,1:T(8,128)(4,1)S(1)} fusion(s32[128]{0:T(128)S(1)} %dynamic_slice.7, s32[128]{0:T(128)S(1)} %dynamic_slice.6, s32[8192]{0:T(1024)S(1)} %bitcast.54), kind=kLoop, calls=%fused_computation.10 | loop fusion | flops 3145728 | bytes 1082368 | tf_op jit(solution)/shard_map/and | solution.py:42
  45.6 123.4 %all-gather.11.cloned.1.call-done = bf16[8192,4,128]{2,0,1:T(8,128)(2,1)} async-done(((bf16[1024,4,128]{2,0,1:T(8,128)(2,1)}), bf16[8192,4,128]{2,0,1:T(8,128)(2,1)}) %all-gather.11.cloned.1.call-update) | async-done | bytes 8388624 | tf_op jit(solution)/shard_map/all_gather | solution.py:79
  169.1 28.2 %fusion.2 = (f32[4,128,4]{1,2,0:T(4,128)S(1)}, f32[4,8192,128,4]{2,1,3,0:T(8,128)}) fusion(pred[128,8192]{0,1:T(8,128)(4,1)S(1)} %compare_and_fusion, bf16[128,4,4,128]{3,2,1,0:T(4,128)(2,1)S(1)} %reshape.125, bf16[8192,4,128]{2,0,1:T(8,128)(2,1)} %all-gather.11.cloned.1.call-done), kind=kOutput, calls=%fused_computation.4 | convolution fusion | flops 4345296896 | bytes 77078528 | tf_op jit(solution)/shard_map/npgd,mgd->gnpm/dot_general | solution.py:39
  197.3 21.4 %fusion = f32[4,128,4]{1,2,0:T(4,128)S(1)} fusion(f32[4,8192,128,4]{2,1,3,0:T(8,128)} %get-tuple-element.10, f32[4,128,4]{1,2,0:T(4,128)S(1)} %get-tuple-element.9, pred[128,8192]{0,1:T(8,128)(4,1)S(1)} %compare_and_fusion), kind=kLoop, calls=%fused_computation.2 | loop fusion | flops 67106816 | bytes 68173824 | tf_op jit(solution)/shard_map/reduce_sum | solution.py:50
  218.7 75.1 %all-gather.7.cloned.1.call-done = bf16[8192,4,128]{0,2,1:T(8,128)(2,1)} async-done(((bf16[1024,4,128]{0,2,1:T(8,128)(2,1)}), bf16[8192,4,128]{0,2,1:T(8,128)(2,1)}) %all-gather.7.cloned.1.call-update) | async-done | bytes 8388624 | tf_op jit(solution)/shard_map/all_gather | solution.py:80
  293.8 27.0 %fusion.19 = bf16[128,4,4,128]{0,3,1,2:T(8,128)(2,1)S(1)} fusion(f32[4,8192,128,4]{2,1,3,0:T(8,128)} %get-tuple-element.10, f32[4,128,4]{1,2,0:T(4,128)S(1)} %get-tuple-element.9, pred[128,8192]{0,1:T(8,128)(4,1)S(1)} %compare_and_fusion, bf16[8192,4,128]{0,2,1:T(8,128)(2,1)} %all-gather.7.cloned.1.call-done, f32[128,4,4]{0,1,2:T(4,128)S(1)} %bitcast.55), kind=kOutput, calls=%fused_computation.14 | convolution fusion | flops 4362600448 | bytes 77086720 | tf_op jit(solution)/shard_map/gnpm,mgd->npgd/dot_general | solution.py:51
  320.8 1.2 copy.21
  (18 shorter events, 0.1 us)
Async XLA Ops:
  6.5 9.8 %copy-start.3 = (f32[128]{0:T(128)S(1)}, f32[128]{0:T(128)}, u32[]{:S(2)}) copy-start(f32[128]{0:T(128)} %param.11) | copy-start | bytes 1540
  6.5 22.9 %all-gather.9.cloned.1.call-start = ((), (), s32[]{:S(2)}) async-start(), calls=%async_computation.2 | async-start | bytes 1572864 | tf_op jit(solution)/shard_map/all_gather | solution.py:75
  17.5 23.7 %copy-start.1 = (s32[1024]{0:T(1024)S(1)}, s32[1024]{0:T(1024)}, u32[]{:S(2)}) copy-start(s32[1024]{0:T(1024)} %param.14) | copy-start | bytes 12292
  17.6 23.7 %copy-start.2 = (s32[1024]{0:T(1024)S(1)}, s32[1024]{0:T(1024)}, u32[]{:S(2)}) copy-start(s32[1024]{0:T(1024)} %param.15) | copy-start | bytes 12292
  17.6 23.7 %copy-start.4 = (s32[32]{0:T(128)S(1)}, s32[32]{0:T(128)}, u32[]{:S(2)}) copy-start(s32[32]{0:T(128)} %param.13) | copy-start | bytes 388
  17.6 24.1 %copy-start = (bf16[128,4,512]{2,1,0:T(4,128)(2,1)S(1)}, bf16[128,4,512]{2,1,0:T(4,128)(2,1)}, u32[]{:S(2)}) copy-start(bf16[128,4,512]{2,1,0:T(4,128)(2,1)} %param.12) | copy-start | bytes 1572868
  17.6 23.6 %all-gather.5.cloned.1.call-start = ((), (), s32[]{:S(2)}) async-start(), calls=%async_computation | async-start | bytes 1572864 | tf_op jit(solution)/shard_map/all_gather | solution.py:76
  28.8 140.3 %all-gather.11.cloned.1.call-start = ((), (), s32[]{:S(2)}) async-start(), calls=%async_computation.3 | async-start | bytes 9437184 | tf_op jit(solution)/shard_map/all_gather | solution.py:79
  29.6 264.2 %all-gather.7.cloned.1.call-start = ((), (), s32[]{:S(2)}) async-start(), calls=%async_computation.1 | async-start | bytes 9437184 | tf_op jit(solution)/shard_map/all_gather | solution.py:80
Sparse Core Ops, SparseCore 0:
  17.7 11.7 all-gather.8
  31.0 10.1 all-gather.4
  43.4 125.6 all-gather.10
  171.1 122.6 all-gather.6
where the time goes:
time: 329 us
  waiting for transfers between devices  211 us (64%)
  matrix products  75.8 us (23%)
  other arithmetic  26.5 us (8%)
  between operations  13.3 us (4%)
    all_gather x1, waiting for transfers between devices, body(): lax.all_gather(pair_keys, 'blk', axis=0, tiled=True)  123 us
    all_gather x1, waiting for transfers between devices, body(): lax.all_gather(pair_values, 'blk', axis=0, tiled=True)  75.1 us
    dot_general x1, matrix products, masked_scores(): jnp.einsum('npgd,mgd->gnpm', query_block, key_block, preferred_element_ty...  28.2 us
    dot_general x1, matrix products, weighted_sum(): jnp.einsum('gnpm,mgd->npgd', weights.astype(jnp.bfloat16), value_block, p...  27 us
    reduce_sum x1, other arithmetic, weighted_sum(): denominator = jnp.sum(weights, axis=3)  21.4 us
    all_gather x1, waiting for transfers between devices, body(): lax.all_gather(value_block, 'section', axis=0, tiled=True)  11.4 us
    dot_general x1, matrix products, make_tables(): jnp.dot(projected, value_weight, preferred_element_type=jnp.float32)  11.2 us
    dot_general x1, matrix products, make_tables(): jnp.dot(projected, key_weight, preferred_element_type=jnp.float32)  9.47 us
  transfers between devices with their start and end apart: 4, of which 4 were waited for; matrix products, arithmetic and copies ran while one was open for 20% of the time, Pallas kernels for 0%

commit v1 on v0

v1 whole, which is shorter than its diff:
```python
import functools
import math

import jax
import jax.numpy as jnp
from jax import lax
from jax.experimental import pallas as pl
from jax.experimental.pallas import tpu as pltpu
from jax.sharding import PartitionSpec as P


HD = 128
FRAMES = 32
EPS = 1e-05
MASKED = -1e30
EXP_SCALE = math.log2(math.e) * HD ** (-0.5)
MIB = 1 << 20
F32 = jnp.float32
BF16 = jnp.bfloat16


def project_kernel(steps, heads, chunk, fetch, *refs):
    x_from, kw_from, vw_from, gain_ref, out_ref = refs[:5]
    x_ref = refs[5] if fetch else x_from
    kw_ref, vw_ref, k_acc, v_acc, sems = refs[6 if fetch else 5 :]
    depth, width = kw_ref.shape
    tile = depth // steps
    columns = pl.ds(chunk * width, width)
    copies = []
    for step in range(steps):
        span = pl.ds(step * tile, tile)
        group = [
            pltpu.make_async_copy(kw_from.at[span, columns], kw_ref.at[span], sems.at[0, step]),
            pltpu.make_async_copy(vw_from.at[span, columns], vw_ref.at[span], sems.at[1, step]),
        ]
        if fetch:
            group.append(
                pltpu.make_async_copy(x_from.at[:, span], x_ref.at[:, span], sems.at[2, step])
            )
        for copy in group:
            copy.start()
        copies.append(group)
    for step in range(steps):
        for copy in copies[step]:
            copy.wait()
        span = slice(step * tile, (step + 1) * tile)
        x = x_ref[:, span]
        k_part = jnp.dot(x, kw_ref[span], preferred_element_type=F32)
        v_part = jnp.dot(x, vw_ref[span], preferred_element_type=F32)
        if step == 0:
            k_acc[...] = k_part
            v_acc[...] = v_part
        else:
            k_acc[...] += k_part
            v_acc[...] += v_part
    for head in range(heads):
        columns = slice(head * HD, (head + 1) * HD)
        raw = k_acc[:, columns]
        mean_square = jnp.mean(raw * raw, axis=1, keepdims=True)
        keys = raw / jnp.sqrt(mean_square + EPS) * gain_ref[...]
        out_ref[head, :, :HD] = keys.astype(BF16)
        out_ref[head, :, HD:] = v_acc[:, columns].astype(BF16)


def project(projected, key_weight, value_weight, gain, chunk, heads, held, keep):
    rows, depth = projected.shape
    steps = 8
    width = heads * HD
    fetch = held is None
    vmem = pl.BlockSpec(memory_space=pltpu.VMEM)
    hbm = pl.BlockSpec(memory_space=pltpu.HBM)
    shape = jax.ShapeDtypeStruct((heads, rows, 2 * HD), BF16)
    x_space = pltpu.VMEM((rows, depth), BF16)
    result = pl.pallas_call(
        functools.partial(project_kernel, steps, heads, chunk, fetch),
        in_specs=[hbm if fetch else vmem, hbm, hbm, vmem],
        out_specs=(vmem, vmem) if keep else vmem,
        out_shape=(shape, x_space) if keep else shape,
        scratch_shapes=([x_space] if fetch and not keep else [])
        + [pltpu.VMEM((depth, width), BF16)] * 2
        + [pltpu.VMEM((rows, width), F32)] * 2
        + [pltpu.SemaphoreType.DMA((3, steps))],
        cost_estimate=pl.CostEstimate(
            flops=4 * rows * depth * width,
            bytes_accessed=2 * depth * (rows * fetch + 2 * width),
            transcendentals=0,
        ),
        compiler_params=pltpu.CompilerParams(vmem_limit_bytes=(50 if fetch else 40) * MIB),
    )(projected if fetch else held, key_weight, value_weight, gain)
    return result if keep else (result, held)


def diagonal():
    rows = lax.broadcasted_iota(jnp.int32, (HD, HD), 0)
    lanes = lax.broadcasted_iota(jnp.int32, (HD, HD), 1)
    return rows == lanes


def to_lanes(column_block, eye):
    return jnp.sum(jnp.where(eye, column_block, 0.0), axis=0, keepdims=True)


def to_column(lane_row, eye):
    return jnp.sum(jnp.where(eye, lane_row, 0.0), axis=1, keepdims=True)


def split_rows(rows):
    high = rows.astype(BF16)
    rest = rows - high.astype(F32)
    middle = rest.astype(BF16)
    low = (rest - middle.astype(F32)).astype(BF16)
    return high, middle, low


def attend_kernel(jobs, mask_count, chunks, sources, heads, *refs):
    group_count = len({group for group, _, _, _ in jobs})
    q_count = 1 + max(query for _, query, _, _ in jobs)
    q_refs, refs = refs[:q_count], refs[q_count:]
    mask_refs, refs = refs[:mask_count], refs[mask_count:]
    kv_refs, refs = refs[: chunks * sources], refs[chunks * sources :]
    frames_ref, refs = refs[0], refs[1:]
    out_refs, (keys, values, *buffers) = refs[:group_count], refs[group_count:]
    rows = q_refs[0].shape[0]
    count = kv_refs[0].shape[1]
    total = sources * count
    tile = min(256, rows)
    block = math.gcd(512, total)

    for slot in range(chunks * heads):
        chunk, head = divmod(slot, heads)
        values[slot, :, HD:] = jnp.ones((total, HD), BF16)
        for source in range(sources):
            span = slice(source * count, (source + 1) * count)
            kv = kv_refs[chunk * sources + source]
            keys[slot, span, :HD] = kv[head, :, :HD]
            keys[slot, span, HD:] = frames_ref[source]
            values[slot, span, :HD] = kv[head, :, HD:]

    eye = diagonal()
    tiles = [
        (group, query, mask, chunk, head, start)
        for group, query, mask, chunk in jobs
        for head in range(heads)
        for start in range(0, rows, tile)
    ]
    lane_rows = {}

    def load_query(index):
        _, query, mask, _, head, start = tiles[index]
        span = slice(start, start + tile)
        columns = slice(head * HD, (head + 1) * HD)
        return jnp.concatenate([q_refs[query][span, columns], mask_refs[mask][span, :]], axis=1)

    def score(index, begin, query):
        _, _, _, chunk, head, _ = tiles[index]
        span = slice(begin, begin + block)
        scores = lax.dot_general(
            query,
            keys[chunk * heads + head, span],
            (((1,), (1,)), ((), ())),
            preferred_element_type=F32,
        )
        buffers[index % 2][:, span] = scores
        top = scores[:, :HD]
        for part in range(HD, block, HD):
            top = jnp.maximum(top, scores[:, part : part + HD])
        return top

    def weigh(index, begin, row_max):
        _, _, _, chunk, head, _ = tiles[index]
        span = slice(begin, begin + block)
        weights = jnp.exp2((buffers[index % 2][:, span] - row_max) * EXP_SCALE)
        return jnp.dot(
            weights.astype(BF16), values[chunk * heads + head, span], preferred_element_type=F32
        )

    def store(index, summed, row_max):
        group, _, _, chunk, head, start = tiles[index]
        out_ref = out_refs[group]
        slot = chunk * heads + head if out_ref.shape[0] > heads else head
        denominator = summed[:, HD:]
        out_ref[slot, start : start + tile, :] = (summed[:, :HD] / denominator).astype(
            out_ref.dtype
        )
        log_sum = row_max * EXP_SCALE + jnp.log2(denominator)
        lanes = lane_rows.setdefault((group, slot), [])
        for part in range(0, tile, HD):
            lanes.append(to_lanes(log_sum[part : part + HD], eye))
        if len(lanes) * HD == rows:
            store_lanes(out_ref, slot, rows, lanes)

    top = None
    query = load_query(0)
    for begin in range(0, total, block):
        part = score(0, begin, query)
        top = part if top is None else jnp.maximum(top, part)
    for index in range(len(tiles)):
        row_max = jnp.max(top, axis=1, keepdims=True)
        ahead = index + 1 < len(tiles)
        if ahead:
            query = load_query(index + 1)
        top = summed = None
        for begin in range(0, total, block):
            if ahead:
                part = score(index + 1, begin, query)
                top = part if top is None else jnp.maximum(top, part)
            part = weigh(index, begin, row_max)
            summed = part if summed is None else summed + part
        store(index, summed, row_max)


def store_lanes(out_ref, slot, rows, lane_rows):
    packed = out_ref.dtype == BF16
    flat = jnp.concatenate(lane_rows, axis=0)
    pieces = [flat]
    if packed:
        pieces = [piece.astype(F32) for piece in split_rows(flat)]
    pad = tail_rows(rows, packed) - len(pieces) * flat.shape[0]
    if pad:
        pieces.append(jnp.zeros((pad, HD), F32))
    out_ref[slot, rows:, :] = jnp.concatenate(pieces, axis=0).astype(out_ref.dtype)


def load_lanes(ref, slot, rows):
    flat = ref[slot, rows:, :].astype(F32)
    count = rows // HD
    if ref.dtype == BF16:
        return flat[:count] + flat[count : 2 * count] + flat[2 * count : 3 * count]
    return flat[:count]


def tail_rows(rows, packed):
    count = rows // HD
    if packed:
        return -(-3 * count // 16) * 16
    return -(-count // 8) * 8


def attend(groups, kv_chunks, frames):
    chunks, sources = len(kv_chunks), len(kv_chunks[0])
    heads, count, _ = kv_chunks[0][0].shape
    rows = groups[0][0][0].shape[0]
    tile = min(256, rows)
    total = sources * count
    jobs, queries = [], []
    for group, (parts, _, _) in enumerate(groups):
        for chunk, part in enumerate(parts):
            jobs.append((group, len(queries), group, chunk))
            queries.append(part)
    slots = chunks * heads
    vmem = pl.BlockSpec(memory_space=pltpu.VMEM)
    inputs = [*queries, *[mask for _, mask, _ in groups], *sum(kv_chunks, []), frames]
    return pl.pallas_call(
        functools.partial(attend_kernel, tuple(jobs), len(groups), chunks, sources, heads),
        in_specs=[vmem] * len(inputs),
        out_specs=[vmem] * len(groups),
        out_shape=[
            jax.ShapeDtypeStruct(
                (slots, rows + tail_rows(rows, packed), HD), BF16 if packed else F32
            )
            for _, _, packed in groups
        ],
        scratch_shapes=[pltpu.VMEM((slots, total, 2 * HD), BF16)] * 2
        + [pltpu.VMEM((tile, total), F32)] * 2,
        cost_estimate=pl.CostEstimate(
            flops=8 * len(groups) * slots * rows * total * HD,
            bytes_accessed=slots * (total * 512 + len(groups) * rows * 512),
            transcendentals=len(groups) * slots * rows * total,
        ),
        compiler_params=pltpu.CompilerParams(vmem_limit_bytes=32 * MIB),
    )(*inputs)


def merge_lanes(lanes):
    top = functools.reduce(jnp.maximum, lanes)
    weights = [jnp.exp2(lane - top) for lane in lanes]
    total = functools.reduce(jnp.add, weights)
    return [weight / total for weight in weights], top + jnp.log2(total)


def merge_slot(refs, slots, rows, eye, write):
    lanes = [load_lanes(ref, slot, rows) for ref, slot in zip(refs, slots)]
    shares, merged_lanes = merge_lanes(lanes)
    for index in range(rows // HD):
        span = slice(index * HD, (index + 1) * HD)
        merged = None
        for ref, slot, share in zip(refs, slots, shares):
            part = to_column(share[index : index + 1], eye) * ref[slot, span, :].astype(F32)
            merged = part if merged is None else merged + part
        write(span, merged)
    return merged_lanes


def merge_kernel(rows, got_ref, own_ref, send_ref):
    eye = diagonal()
    for head in range(send_ref.shape[0]):

        def write(span, merged):
            send_ref[head, span, :] = merged.astype(BF16)

        lanes = merge_slot((got_ref, own_ref), (head, head), rows, eye, write)
        store_lanes(send_ref, head, rows, [lanes])


def merge(got, own, rows):
    return pl.pallas_call(
        functools.partial(merge_kernel, rows),
        out_shape=jax.ShapeDtypeStruct(got.shape, BF16),
        cost_estimate=pl.CostEstimate(
            flops=8 * own.size, bytes_accessed=8 * own.size, transcendentals=0
        ),
        compiler_params=pltpu.CompilerParams(vmem_limit_bytes=32 * MIB),
    )(got, own)


def finish_kernel(chunks, rows, own_ref, *refs):
    out_ref = refs[-1]
    eye = diagonal()
    sub_heads = out_ref.shape[1]
    for slot in range(own_ref.shape[0]):
        chunk, head = divmod(slot, own_ref.shape[0] // chunks)
        columns = slice(slot * HD, (slot + 1) * HD)

        def write(span, merged):
            texts = slice(span.start // sub_heads, span.stop // sub_heads)
            out_ref[texts, :, columns] = merged.reshape(-1, sub_heads, HD).astype(BF16)

        parts = (own_ref, refs[2 * chunk], refs[2 * chunk + 1])
        merge_slot(parts, (slot, head, head), rows, eye, write)


def finish(own, received, rows, shape):
    return pl.pallas_call(
        functools.partial(finish_kernel, len(received), rows),
        out_shape=jax.ShapeDtypeStruct(shape, BF16),
        cost_estimate=pl.CostEstimate(
            flops=8 * own.size, bytes_accessed=8 * own.size, transcendentals=0
        ),
        compiler_params=pltpu.CompilerParams(vmem_limit_bytes=32 * MIB),
        name="finish",
    )(own, *[array for pair in received for array in pair])


def frame_starts(frame_tokens):
    ids = jnp.arange(FRAMES, dtype=jnp.int32)
    before = jnp.where(ids[:, None] < ids[None, :], frame_tokens[:, None], 0)
    return jnp.sum(before, axis=0)


def source_frames(starts, frame_tokens, block, count):
    positions = block * count + jnp.arange(count, dtype=jnp.int32)
    inside = (positions[:, None] >= starts[None, :]) & (
        positions[:, None] < (starts + frame_tokens)[None, :]
    )
    return jnp.pad(inside.astype(BF16), ((0, 0), (0, HD - FRAMES)))


def allowed_frames(span_first, span_count, block, own_rows, sub_heads):
    first = lax.dynamic_slice_in_dim(span_first, block * own_rows, own_rows)[:, None]
    end = jnp.minimum(
        first + lax.dynamic_slice_in_dim(span_count, block * own_rows, own_rows)[:, None], FRAMES
    )
    ids = jnp.arange(HD, dtype=jnp.int32)[None, :]
    blocked = jnp.where((ids >= FRAMES) | ((ids >= first) & (ids < end)), 0.0, MASKED)
    wide = jnp.broadcast_to(blocked.astype(BF16)[:, None, :], (own_rows, sub_heads, HD))
    return wide.reshape(own_rows * sub_heads, HD)


def body(
    projected, key_weight, value_weight, key_gain, queries, frame_tokens, span_first, span_count
):
    own_rows, sub_heads, width = queries.shape
    local_heads = width // HD
    count = projected.shape[0]
    chunk_heads = 2 if local_heads % 2 == 0 else 1
    chunks = local_heads // chunk_heads
    section_count = lax.axis_size("section")
    block_count = lax.axis_size("blk")
    section = lax.axis_index("section")
    block = lax.axis_index("blk")
    bits = block_count.bit_length() - 1
    near, far = 1, 1 << (bits - 1)
    middle = [1 << bit for bit in range(1, bits - 1)]

    def across(x, bit):
        return lax.ppermute(x, "blk", [(i, i ^ bit) for i in range(block_count)])

    def across_section(x):
        return lax.ppermute(
            x, "section", [(i, (i + 1) % section_count) for i in range(section_count)]
        )

    rows = own_rows * sub_heads
    chunk_width = chunk_heads * HD
    own_queries = [
        queries[:, :, c * chunk_width : (c + 1) * chunk_width].reshape(rows, chunk_width)
        for c in range(chunks)
    ]
    far_queries, near_queries, near_far_queries = [], [], []
    for c in range(chunks):
        far_queries.append(across(own_queries[c], far))
        near_queries.append(across(own_queries[c], near))
    for c in range(chunks):
        near_far_queries.append(across(far_queries[c], near))

    starts = frame_starts(frame_tokens)
    source_bits = [0]
    for bit in middle:
        source_bits = source_bits + [other ^ bit for other in source_bits]
    places = [(s, other) for other in source_bits for s in range(section_count)]
    frames = jnp.stack(
        [
            source_frames(
                starts,
                frame_tokens,
                lax.rem(section + section_count - s, section_count) * block_count + (block ^ other),
                count,
            )
            for s, other in places
        ]
    )

    def mask(other):
        return allowed_frames(span_first, span_count, block ^ other, own_rows, sub_heads)

    gain = key_gain.reshape(1, HD)

    received = []
    held = None
    for c in range(chunks):
        own, held = project(
            projected, key_weight, value_weight, gain, c, chunk_heads, held, chunks > 1 and c == 0
        )
        plane = [own]
        for bit in middle:
            plane = plane + [across(part, bit) for part in plane]
        kv_sources = []
        for part in plane:
            kv_sources.append(part)
            if section_count > 1:
                kv_sources.append(across_section(part))
        received.append(kv_sources)

    got_back = []
    for c in range(chunks):
        (corner,) = attend([([near_far_queries[c]], mask(near ^ far), True)], [received[c]], frames)
        got_corner = across(corner, near)
        far_side, near_side = attend(
            [([far_queries[c]], mask(far), False), ([near_queries[c]], mask(near), True)],
            [received[c]],
            frames,
        )
        got_near = across(near_side, near)
        send = merge(got_corner, far_side, rows)
        got_back.append((got_near, across(send, far)))
    (home,) = attend([(own_queries, mask(0), False)], received, frames)
    return finish(home, got_back, rows, queries.shape)


def solution(mesh):
    placed = (
        P(("section", "blk"), None),
        P(None, "head"),
        P(None, "head"),
        P(),
        P("blk", "section", "head"),
        P(),
        P(),
        P(),
    )
    return jax.shard_map(
        body,
        mesh=mesh,
        in_specs=placed,
        out_specs=P("blk", "section", "head"),
        check_vma=False,
    )
```

time: 329 us -> 109 us (0.33)
  waiting for transfers between devices: 211 us -> 40.9 us
  matrix products: 75.8 us -> 0 us
  Pallas kernels: 0 us -> 42.7 us
  other arithmetic: 26.5 us -> 0.85 us
  starting transfers between devices: 0.3 us -> 23.3 us
  between operations: 13.3 us -> 0.28 us
    all_gather x4 -> x0, waiting for transfers between devices: 211 us -> none  [the longest x1 123 us: body(): lax.all_gather(pair_keys, 'blk', axis=0, tiled=True)]
    dot_general x4 -> x0, matrix products: 75.8 us -> none  [the longest x1 28.2 us: masked_scores(): jnp.einsum('npgd,mgd->gnpm', query_block, key_block, preferred_element_ty...]
    pallas_call x0 -> x10, Pallas kernels: none -> 42.7 us  [the longest x5 25.2 us: attend(): pl.pallas_call(functools.partial(attend_kernel, tuple(jobs), len(groups),...]
    ppermute x0 -> x18, waiting for transfers between devices: none -> 40.9 us  [the longest x14 40.9 us: across(): return lax.ppermute(x, 'blk', [(i, i ^ bit) for i in range(block_count)])]
    ppermute x0 -> x18, starting transfers between devices: none -> 23.3 us  [the longest x14 23.2 us: across(): return lax.ppermute(x, 'blk', [(i, i ^ bit) for i in range(block_count)])]
    reduce_sum x2 -> x1, other arithmetic: 21.5 us -> 0.09 us  [frame_starts(): return jnp.sum(before, axis=0)]
    and x1, other arithmetic: 3.73 us -> 0.34 us  [source_frames(): (positions[:, None] >= starts[None, :]) & (positions[:, None] < (starts +...]
  transfers between devices with their start and end apart: 4 -> 18, of which waited for: 4 -> 7; matrix products, arithmetic and copies ran while one was open for 20% -> 1% of each run, Pallas kernels for 0% -> 24%
where the time goes in v1:
time: 109 us
  Pallas kernels  42.7 us (39%)
  waiting for transfers between devices  40.9 us (38%)
  starting transfers between devices  23.3 us (21%)
    ppermute x14, waiting for transfers between devices, across(): return lax.ppermute(x, 'blk', [(i, i ^ bit) for i in range(block_count)])  40.9 us
    pallas_call x5, Pallas kernels, attend(): pl.pallas_call(functools.partial(attend_kernel, tuple(jobs), len(groups),...  25.2 us
    ppermute x14, starting transfers between devices, across(): return lax.ppermute(x, 'blk', [(i, i ^ bit) for i in range(block_count)])  23.2 us
    pallas_call x2, Pallas kernels, project(): pl.pallas_call(functools.partial(project_kernel, steps, heads, chunk, fet...  15 us
  transfers between devices with their start and end apart: 18, of which 7 were waited for; matrix products, arithmetic and copies ran while one was open for 1% of the time, Pallas kernels for 24%

profile of v1, /device:TPU:0, one launch (start us, length us, event | category | flops | bytes accessed | tf_op | source)
XLA Modules:
  0.0 108.7 jit_solution(7446116523606485720)
XLA Ops:
  0.0 8.5 %shard_map.82 = (bf16[2,512,256]{2,1,0:T(8,128)(2,1)}, bf16[512,8192]{1,0:T(8,128)(2,1)S(1)}) custom-call(bf16[512,8192]{1,0:T(8,128)(2,1)} %refs_0_.1, bf16[8192,512]{1,0:T(8,128)(2,1)} %refs_1_.3, bf16[8192,512]{1,0:T(8,128)(2,1)} %refs_2_.3, f32[1,128]{1,0:T(1,128)} %bitcast.20), custom_call_target="tpu_custom_call" | custom-call | flops 4294967296 | bytes 16777216 | tf_op jit(solution)/shard_map/pallas_call | solution.py:74
  8.5 6.6 %shard_map.83.refs_7_.refs_4_.refs_2_ = bf16[2,512,256]{2,1,0:T(8,128)(2,1)S(1)} custom-call(bf16[512,8192]{1,0:T(8,128)(2,1)S(1)} %get-tuple-element.12.refs_0_, bf16[8192,512]{1,0:T(8,128)(2,1)} %refs_1_.3, bf16[8192,512]{1,0:T(8,128)(2,1)} %refs_2_.3, f32[1,128]{1,0:T(1,128)S(1)} %bitcast.21), custom_call_target="tpu_custom_call" | custom-call | flops 4294967296 | bytes 8388608 | tf_op jit(solution)/shard_map/pallas_call | solution.py:74
  15.1 3.1 %collective-permute-start.4 = (bf16[2,512,256]{2,1,0:T(8,128)(2,1)S(1)}, bf16[2,512,256]{2,1,0:T(8,128)(2,1)S(1)}, u32[]{:S(2)}, u32[]{:S(2)}) collective-permute-start(bf16[2,512,256]{2,1,0:T(8,128)(2,1)S(1)} %shard_map.83.refs_7_.refs_4_.refs_2_), channel_id=1, source_target_pairs={{0,4},{2,6},{4,0},{6,2},{8,12},{10,14},{12,8},{14,10},{1,5},{3,7},... | collective-permute-start | bytes 1572872 | tf_op jit(solution)/shard_map/ppermute | solution.py:386
  18.5 2.7 %collective-permute-start.12 = (bf16[512,256]{1,0:T(8,128)(2,1)S(1)}, bf16[512,256]{1,0:T(8,128)(2,1)}, u32[]{:S(2)}, u32[]{:S(2)}) collective-permute-start(bf16[512,256]{1,0:T(8,128)(2,1)S(1)} %reshape.253.refs_1_), channel_id=1, source_target_pairs={{0,8},{2,10},{4,12},{6,14},{8,0},{10,2},{12,4},{14,6},{1,9},{3,11}... | collective-permute-start | bytes 786440 | tf_op jit(solution)/shard_map/ppermute | solution.py:386
  22.4 19.8 %collective-permute-done.4.refs_9_.refs_6_.refs_4_ = bf16[2,512,256]{2,1,0:T(8,128)(2,1)S(1)} collective-permute-done((bf16[2,512,256]{2,1,0:T(8,128)(2,1)S(1)}, bf16[2,512,256]{2,1,0:T(8,128)(2,1)S(1)}, u32[]{:S(2)}, u32[]{:S(2)}) %collective-permute-start.4) | collective-permute-done | bytes 524320 | tf_op jit(solution)/shard_map/ppermute | solution.py:386
  42.5 2.0 %collective-permute-start.15 = (bf16[512,256]{1,0:T(8,128)(2,1)}, bf16[512,256]{1,0:T(8,128)(2,1)S(1)}, u32[]{:S(2)}, u32[]{:S(2)}) collective-permute-start(bf16[512,256]{1,0:T(8,128)(2,1)} %collective-permute-done.12.refs_0_), channel_id=1, source_target_pairs={{0,2},{2,0},{4,6},{6,4},{8,10},{10,8},{12,14},{14,12},{1,3},{3,1},... | collective-permute-start | bytes 786440 | tf_op jit(solution)/shard_map/ppermute | solution.py:386
  44.6 7.3 %collective-permute-done.6.refs_0_ = bf16[512,256]{1,0:T(8,128)(2,1)S(1)} collective-permute-done((bf16[512,256]{1,0:T(8,128)(2,1)S(1)}, bf16[512,256]{1,0:T(8,128)(2,1)S(1)}, u32[]{:S(2)}, u32[]{:S(2)}) %collective-permute-start.6) | collective-permute-done | bytes 262176 | tf_op jit(solution)/shard_map/ppermute | solution.py:386
  51.9 1.5 %collective-permute-start.13 = (bf16[512,256]{1,0:T(8,128)(2,1)S(1)}, bf16[512,256]{1,0:T(8,128)(2,1)S(1)}, u32[]{:S(2)}, u32[]{:S(2)}) collective-permute-start(bf16[512,256]{1,0:T(8,128)(2,1)S(1)} %reshape.253.refs_1_), channel_id=1, source_target_pairs={{0,2},{2,0},{4,6},{6,4},{8,10},{10,8},{12,14},{14,12},{1,3},{3,1},... | collective-permute-start | bytes 786440 | tf_op jit(solution)/shard_map/ppermute | solution.py:386
  54.2 1.5 %collective-permute-start.9 = (bf16[512,256]{1,0:T(8,128)(2,1)S(1)}, bf16[512,256]{1,0:T(8,128)(2,1)S(1)}, u32[]{:S(2)}, u32[]{:S(2)}) collective-permute-start(bf16[512,256]{1,0:T(8,128)(2,1)S(1)} %collective-permute-done.6.refs_0_), channel_id=1, source_target_pairs={{0,2},{2,0},{4,6},{6,4},{8,10},{10,8},{12,14},{14,12},{1,3},{3,1},... | collective-permute-start | bytes 786440 | tf_op jit(solution)/shard_map/ppermute | solution.py:386
  55.8 3.1 %shard_map.89 = bf16[2,528,128]{2,1,0:T(8,128)(2,1)S(1)} custom-call(bf16[512,256]{1,0:T(8,128)(2,1)S(1)} %collective-permute-done.15.refs_0_, bf16[512,128]{1,0:T(8,128)(2,1)S(1)} %bitcast.17, bf16[2,512,256]{2,1,0:T(8,128)(2,1)S(1)} %shard_map.83.refs_7_.refs_4_.refs_2_, bf16[2,512,256]{2,1,0:T(8,128)(2,1)S(1)} %collective-permute-done.3.refs_8_.refs_5_.refs_3_, ...), custom_call_target="tpu_custom_call" | custom-call | flops 2147483648 | bytes 2621440 | tf_op jit(solution)/shard_map/pallas_call | solution.py:253
  58.9 2.2 %collective-permute-done.13.refs_1_ = bf16[512,256]{1,0:T(8,128)(2,1)S(1)} collective-permute-done((bf16[512,256]{1,0:T(8,128)(2,1)S(1)}, bf16[512,256]{1,0:T(8,128)(2,1)S(1)}, u32[]{:S(2)}, u32[]{:S(2)}) %collective-permute-start.13) | collective-permute-done | bytes 262176 | tf_op jit(solution)/shard_map/ppermute | solution.py:386
  61.1 1.5 %collective-permute-start.16 = (bf16[2,528,128]{2,1,0:T(8,128)(2,1)S(1)}, bf16[2,528,128]{2,1,0:T(8,128)(2,1)S(1)}, u32[]{:S(2)}, u32[]{:S(2)}) collective-permute-start(bf16[2,528,128]{2,1,0:T(8,128)(2,1)S(1)} %shard_map.89), channel_id=1, source_target_pairs={{0,2},{2,0},{4,6},{6,4},{8,10},{10,8},{12,14},{14,12},{1,3},{3,1},... | collective-permute-start | bytes 811016 | tf_op jit(solution)/shard_map/ppermute | solution.py:386
  62.7 6.9 %shard_map.88 = (f32[2,520,128]{2,1,0:T(8,128)S(1)}, bf16[2,528,128]{2,1,0:T(8,128)(2,1)S(1)}) custom-call(bf16[512,256]{1,0:T(8,128)(2,1)} %collective-permute-done.12.refs_0_, bf16[512,256]{1,0:T(8,128)(2,1)S(1)} %collective-permute-done.13.refs_1_, bf16[512,128]{1,0:T(8,128)(2,1)S(1)} %bitcast.13, bf16[512,128]{1,0:T(8,128)(2,1)S(1)} %bitcast.15, ...), custom_call_target="tpu_custom_call" | custom-call | flops 4294967296 | bytes 3145728 | tf_op jit(solution)/shard_map/pallas_call | solution.py:253
  70.2 2.2 %collective-permute-done.9.refs_0_ = bf16[512,256]{1,0:T(8,128)(2,1)S(1)} collective-permute-done((bf16[512,256]{1,0:T(8,128)(2,1)S(1)}, bf16[512,256]{1,0:T(8,128)(2,1)S(1)}, u32[]{:S(2)}, u32[]{:S(2)}) %collective-permute-start.9) | collective-permute-done | bytes 262176 | tf_op jit(solution)/shard_map/ppermute | solution.py:386
  72.3 3.1 %shard_map.86 = bf16[2,528,128]{2,1,0:T(8,128)(2,1)S(1)} custom-call(bf16[512,256]{1,0:T(8,128)(2,1)S(1)} %collective-permute-done.9.refs_0_, bf16[512,128]{1,0:T(8,128)(2,1)S(1)} %bitcast.18, bf16[2,512,256]{2,1,0:T(8,128)(2,1)S(1)} %copy-done.1, bf16[2,512,256]{2,1,0:T(8,128)(2,1)S(1)} %collective-permute-done.refs_4_.refs_5_.refs_3_, ...), custom_call_target="tpu_custom_call" | custom-call | flops 2147483648 | bytes 2621440 | tf_op jit(solution)/shard_map/pallas_call | solution.py:253
  75.5 1.6 %collective-permute-start.10 = (bf16[2,528,128]{2,1,0:T(8,128)(2,1)S(1)}, bf16[2,528,128]{2,1,0:T(8,128)(2,1)S(1)}, u32[]{:S(2)}, u32[]{:S(2)}) collective-permute-start(bf16[2,528,128]{2,1,0:T(8,128)(2,1)S(1)} %shard_map.86), channel_id=1, source_target_pairs={{0,2},{2,0},{4,6},{6,4},{8,10},{10,8},{12,14},{14,12},{1,3},{3,1},... | collective-permute-start | bytes 811016 | tf_op jit(solution)/shard_map/ppermute | solution.py:386
  77.0 5.9 %shard_map.85 = (f32[2,520,128]{2,1,0:T(8,128)S(1)}, bf16[2,528,128]{2,1,0:T(8,128)(2,1)S(1)}) custom-call(bf16[512,256]{1,0:T(8,128)(2,1)S(1)} %collective-permute-done.6.refs_0_, bf16[512,256]{1,0:T(8,128)(2,1)S(1)} %collective-permute-done.7.refs_1_, bf16[512,128]{1,0:T(8,128)(2,1)S(1)} %bitcast.14, bf16[512,128]{1,0:T(8,128)(2,1)S(1)} %bitcast.16, ...), custom_call_target="tpu_custom_call" | custom-call | flops 4294967296 | bytes 3145728 | tf_op jit(solution)/shard_map/pallas_call | solution.py:253
  83.9 3.4 %collective-permute-start.17 = (bf16[2,528,128]{2,1,0:T(8,128)(2,1)S(1)}, bf16[2,528,128]{2,1,0:T(8,128)(2,1)S(1)}, u32[]{:S(2)}, u32[]{:S(2)}) collective-permute-start(bf16[2,528,128]{2,1,0:T(8,128)(2,1)S(1)} %shard_map.90), channel_id=1, source_target_pairs={{0,8},{2,10},{4,12},{6,14},{8,0},{10,2},{12,4},{14,6},{1,9},{3,11}... | collective-permute-start | bytes 811016 | tf_op jit(solution)/shard_map/ppermute | solution.py:386
  87.4 2.3 %collective-permute-done.10.got_ref = bf16[2,528,128]{2,1,0:T(8,128)(2,1)S(1)} collective-permute-done((bf16[2,528,128]{2,1,0:T(8,128)(2,1)S(1)}, bf16[2,528,128]{2,1,0:T(8,128)(2,1)S(1)}, u32[]{:S(2)}, u32[]{:S(2)}) %collective-permute-start.10) | collective-permute-done | bytes 270368 | tf_op jit(solution)/shard_map/ppermute | solution.py:386
  90.1 3.4 %collective-permute-start.11 = (bf16[2,528,128]{2,1,0:T(8,128)(2,1)S(1)}, bf16[2,528,128]{2,1,0:T(8,128)(2,1)S(1)}, u32[]{:S(2)}, u32[]{:S(2)}) collective-permute-start(bf16[2,528,128]{2,1,0:T(8,128)(2,1)S(1)} %shard_map.87), channel_id=1, source_target_pairs={{0,8},{2,10},{4,12},{6,14},{8,0},{10,2},{12,4},{14,6},{1,9},{3,11}... | collective-permute-start | bytes 811016 | tf_op jit(solution)/shard_map/ppermute | solution.py:386
  93.6 6.2 %shard_map.84.own_ref = f32[4,520,128]{2,1,0:T(8,128)S(1)} custom-call(bf16[512,256]{1,0:T(8,128)(2,1)S(1)} %reshape.252.refs_0_, bf16[512,256]{1,0:T(8,128)(2,1)S(1)} %reshape.253.refs_1_, bf16[512,128]{1,0:T(8,128)(2,1)S(1)} %bitcast.19, bf16[2,512,256]{2,1,0:T(8,128)(2,1)S(1)} %copy-done.1, ...), custom_call_target="tpu_custom_call" | custom-call | flops 4294967296 | bytes 5242880 | tf_op jit(solution)/shard_map/pallas_call | solution.py:253
  99.8 3.3 %collective-permute-done.17.refs_3_ = bf16[2,528,128]{2,1,0:T(8,128)(2,1)S(1)} collective-permute-done((bf16[2,528,128]{2,1,0:T(8,128)(2,1)S(1)}, bf16[2,528,128]{2,1,0:T(8,128)(2,1)S(1)}, u32[]{:S(2)}, u32[]{:S(2)}) %collective-permute-start.17) | collective-permute-done | bytes 270368 | tf_op jit(solution)/shard_map/ppermute | solution.py:386
  103.1 3.8 %collective-permute-done.11.refs_1_ = bf16[2,528,128]{2,1,0:T(8,128)(2,1)S(1)} collective-permute-done((bf16[2,528,128]{2,1,0:T(8,128)(2,1)S(1)}, bf16[2,528,128]{2,1,0:T(8,128)(2,1)S(1)}, u32[]{:S(2)}, u32[]{:S(2)}) %collective-permute-start.11) | collective-permute-done | bytes 270368 | tf_op jit(solution)/shard_map/ppermute | solution.py:386
  107.0 1.7 %finish.1 = bf16[128,4,512]{2,1,0:T(4,128)(2,1)} custom-call(f32[4,520,128]{2,1,0:T(8,128)S(1)} %shard_map.84.own_ref, bf16[2,528,128]{2,1,0:T(8,128)(2,1)S(1)} %collective-permute-done.8.refs_0_, bf16[2,528,128]{2,1,0:T(8,128)(2,1)S(1)} %collective-permute-done.11.refs_1_, bf16[2,528,128]{2,1,0:T(8,128)(2,1)S(1)} %collective-permute-done.14.refs_2_, ...), custom_call_target="tpu_custom_call" | custom-call | flops 2129920 | bytes 2129920 | tf_op jit(solution)/shard_map/finish/pallas_call | solution.py:333
  (54 shorter events, 4.7 us)
Async XLA Ops:
  0.0 8.5 %copy-start = (f32[128]{0:T(128)S(1)}, f32[128]{0:T(128)}, u32[]{:S(2)}) copy-start(f32[128]{0:T(128)} %param.11) | copy-start | bytes 1540
  8.5 9.8 %copy-start.2 = (bf16[128,4,512]{2,1,0:T(4,128)(2,1)S(1)}, bf16[128,4,512]{2,1,0:T(4,128)(2,1)}, u32[]{:S(2)}) copy-start(bf16[128,4,512]{2,1,0:T(4,128)(2,1)} %param.12) | copy-start | bytes 1572868
  8.5 12.7 %copy-start.1 = (bf16[2,512,256]{2,1,0:T(8,128)(2,1)S(1)}, bf16[2,512,256]{2,1,0:T(8,128)(2,1)}, u32[]{:S(2)}) copy-start(bf16[2,512,256]{2,1,0:T(8,128)(2,1)} %get-tuple-element.11.refs_3_.refs_4_.refs_2_) | copy-start | bytes 1572868
  8.5 13.3 %copy-start.5 = (s32[32]{0:T(128)S(1)}, s32[32]{0:T(128)}, u32[]{:S(2)}) copy-start(s32[32]{0:T(128)} %param.13) | copy-start | bytes 388
  8.5 13.5 %copy-start.3 = (s32[1024]{0:T(1024)S(1)}, s32[1024]{0:T(1024)}, u32[]{:S(2)}) copy-start(s32[1024]{0:T(1024)} %param.15) | copy-start | bytes 12292
  8.5 13.5 %copy-start.4 = (s32[1024]{0:T(1024)S(1)}, s32[1024]{0:T(1024)}, u32[]{:S(2)}) copy-start(s32[1024]{0:T(1024)} %param.14) | copy-start | bytes 12292
  15.1 27.1 %collective-permute-start.4 = (bf16[2,512,256]{2,1,0:T(8,128)(2,1)S(1)}, bf16[2,512,256]{2,1,0:T(8,128)(2,1)S(1)}, u32[]{:S(2)}, u32[]{:S(2)}) collective-permute-start(bf16[2,512,256]{2,1,0:T(8,128)(2,1)S(1)} %shard_map.83.refs_7_.refs_4_.refs_2_), channel_id=1, source_target_pairs={{0,4},{2,6},{4,0},{6,2},{8,12},{10,14},{12,8},{14,10},{1,5},{3,7},... | collective-permute-start | bytes 1572872 | tf_op jit(solution)/shard_map/ppermute | solution.py:386
  18.2 35.3 %collective-permute-start.3 = (bf16[2,512,256]{2,1,0:T(8,128)(2,1)S(1)}, bf16[2,512,256]{2,1,0:T(8,128)(2,1)S(1)}, u32[]{:S(2)}, u32[]{:S(2)}) collective-permute-start(bf16[2,512,256]{2,1,0:T(8,128)(2,1)S(1)} %shard_map.83.refs_7_.refs_4_.refs_2_), channel_id=1, source_target_pairs={{0,16},{16,0},{1,17},{17,1},{2,18},{18,2},{3,19},{19,3},{4,20},{20... | collective-permute-start | bytes 1572872 | tf_op jit(solution)/shard_map/ppermute | solution.py:389
  18.5 24.0 %collective-permute-start.12 = (bf16[512,256]{1,0:T(8,128)(2,1)S(1)}, bf16[512,256]{1,0:T(8,128)(2,1)}, u32[]{:S(2)}, u32[]{:S(2)}) collective-permute-start(bf16[512,256]{1,0:T(8,128)(2,1)S(1)} %reshape.253.refs_1_), channel_id=1, source_target_pairs={{0,8},{2,10},{4,12},{6,14},{8,0},{10,2},{12,4},{14,6},{1,9},{3,11}... | collective-permute-start | bytes 786440 | tf_op jit(solution)/shard_map/ppermute | solution.py:386
  21.1 33.1 %collective-permute-start.1 = (bf16[2,512,256]{2,1,0:T(8,128)(2,1)S(1)}, bf16[2,512,256]{2,1,0:T(8,128)(2,1)S(1)}, u32[]{:S(2)}, u32[]{:S(2)}) collective-permute-start(bf16[2,512,256]{2,1,0:T(8,128)(2,1)S(1)} %copy-done.1), channel_id=1, source_target_pairs={{0,4},{2,6},{4,0},{6,2},{8,12},{10,14},{12,8},{14,10},{1,5},{3,7},... | collective-permute-start | bytes 1572872 | tf_op jit(solution)/shard_map/ppermute | solution.py:386
  21.7 30.3 %collective-permute-start.6 = (bf16[512,256]{1,0:T(8,128)(2,1)S(1)}, bf16[512,256]{1,0:T(8,128)(2,1)S(1)}, u32[]{:S(2)}, u32[]{:S(2)}) collective-permute-start(bf16[512,256]{1,0:T(8,128)(2,1)S(1)} %reshape.252.refs_0_), channel_id=1, source_target_pairs={{0,8},{2,10},{4,12},{6,14},{8,0},{10,2},{12,4},{14,6},{1,9},{3,11}... | collective-permute-start | bytes 786440 | tf_op jit(solution)/shard_map/ppermute | solution.py:386
  42.2 13.5 %collective-permute-start.5 = (bf16[2,512,256]{2,1,0:T(8,128)(2,1)S(1)}, bf16[2,512,256]{2,1,0:T(8,128)(2,1)S(1)}, u32[]{:S(2)}, u32[]{:S(2)}) collective-permute-start(bf16[2,512,256]{2,1,0:T(8,128)(2,1)S(1)} %collective-permute-done.4.refs_9_.refs_6_.refs_4_), channel_id=1, source_target_pairs={{0,16},{16,0},{1,17},{17,1},{2,18},{18,2},{3,19},{19,3},{4,20},{20... | collective-permute-start | bytes 1572872 | tf_op jit(solution)/shard_map/ppermute | solution.py:389
  42.5 11.2 %collective-permute-start.15 = (bf16[512,256]{1,0:T(8,128)(2,1)}, bf16[512,256]{1,0:T(8,128)(2,1)S(1)}, u32[]{:S(2)}, u32[]{:S(2)}) collective-permute-start(bf16[512,256]{1,0:T(8,128)(2,1)} %collective-permute-done.12.refs_0_), channel_id=1, source_target_pairs={{0,2},{2,0},{4,6},{6,4},{8,10},{10,8},{12,14},{14,12},{1,3},{3,1},... | collective-permute-start | bytes 786440 | tf_op jit(solution)/shard_map/ppermute | solution.py:386
  51.9 9.2 %collective-permute-start.13 = (bf16[512,256]{1,0:T(8,128)(2,1)S(1)}, bf16[512,256]{1,0:T(8,128)(2,1)S(1)}, u32[]{:S(2)}, u32[]{:S(2)}) collective-permute-start(bf16[512,256]{1,0:T(8,128)(2,1)S(1)} %reshape.253.refs_1_), channel_id=1, source_target_pairs={{0,2},{2,0},{4,6},{6,4},{8,10},{10,8},{12,14},{14,12},{1,3},{3,1},... | collective-permute-start | bytes 786440 | tf_op jit(solution)/shard_map/ppermute | solution.py:386
  53.6 16.0 %collective-permute-start = (bf16[2,512,256]{2,1,0:T(8,128)(2,1)S(1)}, bf16[2,512,256]{2,1,0:T(8,128)(2,1)S(1)}, u32[]{:S(2)}, u32[]{:S(2)}) collective-permute-start(bf16[2,512,256]{2,1,0:T(8,128)(2,1)S(1)} %copy-done.1), channel_id=1, source_target_pairs={{0,16},{16,0},{1,17},{17,1},{2,18},{18,2},{3,19},{19,3},{4,20},{20... | collective-permute-start | bytes 1572872 | tf_op jit(solution)/shard_map/ppermute | solution.py:389
  53.7 23.4 %collective-permute-start.7 = (bf16[512,256]{1,0:T(8,128)(2,1)S(1)}, bf16[512,256]{1,0:T(8,128)(2,1)S(1)}, u32[]{:S(2)}, u32[]{:S(2)}) collective-permute-start(bf16[512,256]{1,0:T(8,128)(2,1)S(1)} %reshape.252.refs_0_), channel_id=1, source_target_pairs={{0,2},{2,0},{4,6},{6,4},{8,10},{10,8},{12,14},{14,12},{1,3},{3,1},... | collective-permute-start | bytes 786440 | tf_op jit(solution)/shard_map/ppermute | solution.py:386
  54.2 18.1 %collective-permute-start.9 = (bf16[512,256]{1,0:T(8,128)(2,1)S(1)}, bf16[512,256]{1,0:T(8,128)(2,1)S(1)}, u32[]{:S(2)}, u32[]{:S(2)}) collective-permute-start(bf16[512,256]{1,0:T(8,128)(2,1)S(1)} %collective-permute-done.6.refs_0_), channel_id=1, source_target_pairs={{0,2},{2,0},{4,6},{6,4},{8,10},{10,8},{12,14},{14,12},{1,3},{3,1},... | collective-permute-start | bytes 786440 | tf_op jit(solution)/shard_map/ppermute | solution.py:386
  55.7 16.6 %collective-permute-start.2 = (bf16[2,512,256]{2,1,0:T(8,128)(2,1)S(1)}, bf16[2,512,256]{2,1,0:T(8,128)(2,1)S(1)}, u32[]{:S(2)}, u32[]{:S(2)}) collective-permute-start(bf16[2,512,256]{2,1,0:T(8,128)(2,1)S(1)} %collective-permute-done.1.refs_5_.refs_6_.refs_4_), channel_id=1, source_target_pairs={{0,16},{16,0},{1,17},{17,1},{2,18},{18,2},{3,19},{19,3},{4,20},{20... | collective-permute-start | bytes 1572872 | tf_op jit(solution)/shard_map/ppermute | solution.py:389
  61.1 22.5 %collective-permute-start.16 = (bf16[2,528,128]{2,1,0:T(8,128)(2,1)S(1)}, bf16[2,528,128]{2,1,0:T(8,128)(2,1)S(1)}, u32[]{:S(2)}, u32[]{:S(2)}) collective-permute-start(bf16[2,528,128]{2,1,0:T(8,128)(2,1)S(1)} %shard_map.89), channel_id=1, source_target_pairs={{0,2},{2,0},{4,6},{6,4},{8,10},{10,8},{12,14},{14,12},{1,3},{3,1},... | collective-permute-start | bytes 811016 | tf_op jit(solution)/shard_map/ppermute | solution.py:386
  69.6 30.2 %collective-permute-start.14 = (bf16[2,528,128]{2,1,0:T(8,128)(2,1)S(1)}, bf16[2,528,128]{2,1,0:T(8,128)(2,1)S(1)}, u32[]{:S(2)}, u32[]{:S(2)}) collective-permute-start(bf16[2,528,128]{2,1,0:T(8,128)(2,1)S(1)} %get-tuple-element.15), channel_id=1, source_target_pairs={{0,2},{2,0},{4,6},{6,4},{8,10},{10,8},{12,14},{14,12},{1,3},{3,1},... | collective-permute-start | bytes 811016 | tf_op jit(solution)/shard_map/ppermute | solution.py:386
  75.5 14.3 %collective-permute-start.10 = (bf16[2,528,128]{2,1,0:T(8,128)(2,1)S(1)}, bf16[2,528,128]{2,1,0:T(8,128)(2,1)S(1)}, u32[]{:S(2)}, u32[]{:S(2)}) collective-permute-start(bf16[2,528,128]{2,1,0:T(8,128)(2,1)S(1)} %shard_map.86), channel_id=1, source_target_pairs={{0,2},{2,0},{4,6},{6,4},{8,10},{10,8},{12,14},{14,12},{1,3},{3,1},... | collective-permute-start | bytes 811016 | tf_op jit(solution)/shard_map/ppermute | solution.py:386
  83.0 16.8 %collective-permute-start.8 = (bf16[2,528,128]{2,1,0:T(8,128)(2,1)S(1)}, bf16[2,528,128]{2,1,0:T(8,128)(2,1)S(1)}, u32[]{:S(2)}, u32[]{:S(2)}) collective-permute-start(bf16[2,528,128]{2,1,0:T(8,128)(2,1)S(1)} %get-tuple-element.13), channel_id=1, source_target_pairs={{0,2},{2,0},{4,6},{6,4},{8,10},{10,8},{12,14},{14,12},{1,3},{3,1},... | collective-permute-start | bytes 811016 | tf_op jit(solution)/shard_map/ppermute | solution.py:386
  83.9 19.2 %collective-permute-start.17 = (bf16[2,528,128]{2,1,0:T(8,128)(2,1)S(1)}, bf16[2,528,128]{2,1,0:T(8,128)(2,1)S(1)}, u32[]{:S(2)}, u32[]{:S(2)}) collective-permute-start(bf16[2,528,128]{2,1,0:T(8,128)(2,1)S(1)} %shard_map.90), channel_id=1, source_target_pairs={{0,8},{2,10},{4,12},{6,14},{8,0},{10,2},{12,4},{14,6},{1,9},{3,11}... | collective-permute-start | bytes 811016 | tf_op jit(solution)/shard_map/ppermute | solution.py:386
  90.1 16.9 %collective-permute-start.11 = (bf16[2,528,128]{2,1,0:T(8,128)(2,1)S(1)}, bf16[2,528,128]{2,1,0:T(8,128)(2,1)S(1)}, u32[]{:S(2)}, u32[]{:S(2)}) collective-permute-start(bf16[2,528,128]{2,1,0:T(8,128)(2,1)S(1)} %shard_map.87), channel_id=1, source_target_pairs={{0,8},{2,10},{4,12},{6,14},{8,0},{10,2},{12,4},{14,6},{1,9},{3,11}... | collective-permute-start | bytes 811016 | tf_op jit(solution)/shard_map/ppermute | solution.py:386

commit v2 on v1

--- a/solution.py
+++ b/solution.py
@@ -71,6 +71,10 @@
     hbm = pl.BlockSpec(memory_space=pltpu.HBM)
     shape = jax.ShapeDtypeStruct((heads, rows, 2 * HD), BF16)
     x_space = pltpu.VMEM((rows, depth), BF16)
+    stay = functools.partial(pltpu.with_memory_space_constraint, memory_space=pltpu.HBM)
+    key_weight, value_weight = stay(key_weight), stay(value_weight)
+    if fetch:
+        projected = stay(projected)
     result = pl.pallas_call(
         functools.partial(project_kernel, steps, heads, chunk, fetch),
         in_specs=[hbm if fetch else vmem, hbm, hbm, vmem],
@@ -85,7 +89,7 @@
             bytes_accessed=2 * depth * (rows * fetch + 2 * width),
             transcendentals=0,
         ),
-        compiler_params=pltpu.CompilerParams(vmem_limit_bytes=(50 if fetch else 40) * MIB),
+        compiler_params=pltpu.CompilerParams(vmem_limit_bytes=24 * MIB),
     )(projected if fetch else held, key_weight, value_weight, gain)
     return result if keep else (result, held)
 
@@ -112,51 +116,81 @@
     return high, middle, low
 
 
-def attend_kernel(jobs, mask_count, chunks, sources, heads, *refs):
-    group_count = len({group for group, _, _, _ in jobs})
-    q_count = 1 + max(query for _, query, _, _ in jobs)
-    q_refs, refs = refs[:q_count], refs[q_count:]
-    mask_refs, refs = refs[:mask_count], refs[mask_count:]
-    kv_refs, refs = refs[: chunks * sources], refs[chunks * sources :]
-    frames_ref, refs = refs[0], refs[1:]
-    out_refs, (keys, values, *buffers) = refs[:group_count], refs[group_count:]
+def build_tables(heads, places, kv_refs, edges_ref, keys, values):
+    sources = len(kv_refs)
+    count = kv_refs[0].shape[1]
+    section_count, block_count = lax.axis_size("section"), lax.axis_size("blk")
+    section, row_block = lax.axis_index("section"), lax.axis_index("blk")
+    values[:, :, HD:] = jnp.ones((heads, sources * count, HD), BF16)
+    for source, kv in enumerate(kv_refs):
+        other, back = places[source]
+        place = lax.rem(section + section_count - back, section_count) * block_count
+        base = (place + (row_block ^ other)) * count
+        span = slice(source * count, (source + 1) * count)
+        token = base + lax.broadcasted_iota(jnp.int32, (count, HD), 0)
+        inside = (token >= edges_ref[0:1, :]) & (token < edges_ref[1:2, :])
+        frame = jnp.where(inside, 1.0, 0.0).astype(BF16)
+        for head in range(heads):
+            keys[head, span, :HD] = kv[head, :, :HD]
+            keys[head, span, HD:] = frame
+            values[head, span, :HD] = kv[head, :, HD:]
+
+
+def build_mask(other, sub_heads, first_ref, count_ref, mask):
+    text_rows = first_ref.shape[1]
+    row = lax.axis_index("blk") ^ other
+    eye = diagonal()
+    frame = lax.broadcasted_iota(jnp.int32, (HD, HD), 1).astype(F32)
+    for start in range(0, text_rows, HD):
+        span = slice(start, start + HD)
+        first = to_column(first_ref[pl.ds(row, 1), span].astype(F32), eye)
+        end = first + to_column(count_ref[pl.ds(row, 1), span].astype(F32), eye)
+        seen = (frame >= first) & (frame < end) | (frame >= FRAMES)
+        blocked = jnp.where(seen, 0.0, MASKED)[:, None, :]
+        wide = jnp.broadcast_to(blocked, (HD, sub_heads, HD)).reshape(HD * sub_heads, HD)
+        mask[start * sub_heads : (start + HD) * sub_heads, :] = wide.astype(BF16)
+
+
+def attend_kernel(others, places, heads, *refs):
+    group_count = len(others)
+    q_refs, refs = refs[:group_count], refs[group_count:]
+    (first_ref, count_ref, *refs), mask_refs = refs[:-1], refs[-1]
+    if places:
+        kv_refs, refs = refs[: len(places)], refs[len(places) :]
+        edges_ref, *refs = refs
+        out_refs, (keys, values, *buffers) = refs[:group_count], refs[group_count:]
+        build_tables(keys.shape[0], places, kv_refs, edges_ref, keys, values)
+    else:
+        keys, values, *refs = refs
+        out_refs, buffers = refs[:group_count], refs[group_count:]
     rows = q_refs[0].shape[0]
-    count = kv_refs[0].shape[1]
-    total = sources * count
+    total = keys.shape[1]
     tile = min(256, rows)
     block = math.gcd(512, total)
-
-    for slot in range(chunks * heads):
-        chunk, head = divmod(slot, heads)
-        values[slot, :, HD:] = jnp.ones((total, HD), BF16)
-        for source in range(sources):
-            span = slice(source * count, (source + 1) * count)
-            kv = kv_refs[chunk * sources + source]
-            keys[slot, span, :HD] = kv[head, :, :HD]
-            keys[slot, span, HD:] = frames_ref[source]
-            values[slot, span, :HD] = kv[head, :, HD:]
+    for group, other in enumerate(others):
+        build_mask(other, rows // first_ref.shape[1], first_ref, count_ref, mask_refs.at[group])
 
     eye = diagonal()
     tiles = [
-        (group, query, mask, chunk, head, start)
-        for group, query, mask, chunk in jobs
-        for head in range(heads)
+        (group, head, start)
+        for group in range(len(others))
+        for head in heads
         for start in range(0, rows, tile)
     ]
     lane_rows = {}
 
     def load_query(index):
-        _, query, mask, _, head, start = tiles[index]
+        group, head, start = tiles[index]
         span = slice(start, start + tile)
         columns = slice(head * HD, (head + 1) * HD)
-        return jnp.concatenate([q_refs[query][span, columns], mask_refs[mask][span, :]], axis=1)
+        return jnp.concatenate([q_refs[group][span, columns], mask_refs[group, span, :]], axis=1)
 
     def score(index, begin, query):
-        _, _, _, chunk, head, _ = tiles[index]
+        _, head, _ = tiles[index]
         span = slice(begin, begin + block)
         scores = lax.dot_general(
             query,
-            keys[chunk * heads + head, span],
+            keys[head, span],
             (((1,), (1,)), ((), ())),
             preferred_element_type=F32,
         )
@@ -167,17 +201,17 @@
         return top
 
     def weigh(index, begin, row_max):
-        _, _, _, chunk, head, _ = tiles[index]
+        _, head, _ = tiles[index]
         span = slice(begin, begin + block)
         weights = jnp.exp2((buffers[index % 2][:, span] - row_max) * EXP_SCALE)
         return jnp.dot(
-            weights.astype(BF16), values[chunk * heads + head, span], preferred_element_type=F32
+            weights.astype(BF16), values[head, span], preferred_element_type=F32
         )
 
     def store(index, summed, row_max):
-        group, _, _, chunk, head, start = tiles[index]
+        group, head, start = tiles[index]
         out_ref = out_refs[group]
-        slot = chunk * heads + head if out_ref.shape[0] > heads else head
+        slot = heads.index(head)
         denominator = summed[:, HD:]
         out_ref[slot, start : start + tile, :] = (summed[:, :HD] / denominator).astype(
             out_ref.dtype
@@ -236,32 +270,39 @@
     return -(-count // 8) * 8
 
 
-def attend(groups, kv_chunks, frames):
-    chunks, sources = len(kv_chunks), len(kv_chunks[0])
-    heads, count, _ = kv_chunks[0][0].shape
-    rows = groups[0][0][0].shape[0]
+def attend(groups, spans, tables, heads, kv_sources=None, edges=None, places=()):
+    build = kv_sources is not None
+    if build:
+        table_heads, count, _ = kv_sources[0].shape
+        total = len(kv_sources) * count
+    else:
+        total = tables[0].shape[1]
+    rows = groups[0][0].shape[0]
     tile = min(256, rows)
-    total = sources * count
-    jobs, queries = [], []
-    for group, (parts, _, _) in enumerate(groups):
-        for chunk, part in enumerate(parts):
-            jobs.append((group, len(queries), group, chunk))
-            queries.append(part)
-    slots = chunks * heads
+    queries = [part for part, _, _ in groups]
+    slots = len(heads)
     vmem = pl.BlockSpec(memory_space=pltpu.VMEM)
-    inputs = [*queries, *[mask for _, mask, _ in groups], *sum(kv_chunks, []), frames]
+    inputs = [*queries, *spans]
+    inputs += [*kv_sources, edges] if build else list(tables)
+    in_specs = [vmem] * len(inputs)
+    out_shape = [
+        jax.ShapeDtypeStruct((slots, rows + tail_rows(rows, packed), HD), BF16 if packed else F32)
+        for _, _, packed in groups
+    ]
+    if build:
+        out_shape += [pltpu.VMEM((table_heads, total, 2 * HD), BF16)] * 2
     return pl.pallas_call(
-        functools.partial(attend_kernel, tuple(jobs), len(groups), chunks, sources, heads),
-        in_specs=[vmem] * len(inputs),
-        out_specs=[vmem] * len(groups),
-        out_shape=[
-            jax.ShapeDtypeStruct(
-                (slots, rows + tail_rows(rows, packed), HD), BF16 if packed else F32
-            )
-            for _, _, packed in groups
-        ],
-        scratch_shapes=[pltpu.VMEM((slots, total, 2 * HD), BF16)] * 2
-        + [pltpu.VMEM((tile, total), F32)] * 2,
+        functools.partial(
+            attend_kernel,
+            tuple(other for _, other, _ in groups),
+            tuple(places),
+            tuple(heads),
+        ),
+        in_specs=in_specs,
+        out_specs=[vmem] * len(out_shape),
+        out_shape=out_shape,
+        scratch_shapes=[pltpu.VMEM((tile, total), F32)] * 2
+        + [pltpu.VMEM((len(groups), rows, HD), BF16)],
         cost_estimate=pl.CostEstimate(
             flops=8 * len(groups) * slots * rows * total * HD,
             bytes_accessed=slots * (total * 512 + len(groups) * rows * 512),
@@ -313,57 +354,66 @@
     )(got, own)
 
 
-def finish_kernel(chunks, rows, own_ref, *refs):
+def slots_of(refs):
+    return [(ref, head) for ref in refs for head in range(ref.shape[0])]
+
+
+def gather_home_kernel(count, rows, *refs):
+    out_ref = refs[-1]
+    eye = diagonal()
+    pairs = zip(slots_of(refs[:count]), slots_of(refs[count:-1]))
+    for slot, ((own, own_head), (got, got_head)) in enumerate(pairs):
+
+        def write(span, merged):
+            out_ref[slot, span, :] = merged
+
+        lanes = merge_slot((own, got), (own_head, got_head), rows, eye, write)
+        store_lanes(out_ref, slot, rows, [lanes])
+
+
+def gather_home(own, received, rows):
+    slots = sum(part.shape[0] for part in own)
+    return pl.pallas_call(
+        functools.partial(gather_home_kernel, len(own), rows),
+        out_shape=jax.ShapeDtypeStruct((slots, *own[0].shape[1:]), F32),
+        cost_estimate=pl.CostEstimate(
+            flops=8 * slots * rows * HD, bytes_accessed=8 * slots * rows * HD, transcendentals=0
+        ),
+        compiler_params=pltpu.CompilerParams(vmem_limit_bytes=32 * MIB),
+        name="gather_home",
+    )(*own, *received)
+
+
+def finish_kernel(rows, own_ref, *refs):
     out_ref = refs[-1]
     eye = diagonal()
     sub_heads = out_ref.shape[1]
-    for slot in range(own_ref.shape[0]):
-        chunk, head = divmod(slot, own_ref.shape[0] // chunks)
+    for slot, (got, got_head) in enumerate(slots_of(refs[:-1])):
         columns = slice(slot * HD, (slot + 1) * HD)
 
         def write(span, merged):
             texts = slice(span.start // sub_heads, span.stop // sub_heads)
             out_ref[texts, :, columns] = merged.reshape(-1, sub_heads, HD).astype(BF16)
 
-        parts = (own_ref, refs[2 * chunk], refs[2 * chunk + 1])
-        merge_slot(parts, (slot, head, head), rows, eye, write)
+        merge_slot((own_ref, got), (slot, got_head), rows, eye, write)
 
 
 def finish(own, received, rows, shape):
     return pl.pallas_call(
-        functools.partial(finish_kernel, len(received), rows),
+        functools.partial(finish_kernel, rows),
         out_shape=jax.ShapeDtypeStruct(shape, BF16),
         cost_estimate=pl.CostEstimate(
             flops=8 * own.size, bytes_accessed=8 * own.size, transcendentals=0
         ),
         compiler_params=pltpu.CompilerParams(vmem_limit_bytes=32 * MIB),
         name="finish",
-    )(own, *[array for pair in received for array in pair])
+    )(own, *received)
 
 
 def frame_starts(frame_tokens):
     ids = jnp.arange(FRAMES, dtype=jnp.int32)
     before = jnp.where(ids[:, None] < ids[None, :], frame_tokens[:, None], 0)
     return jnp.sum(before, axis=0)
-
-
-def source_frames(starts, frame_tokens, block, count):
-    positions = block * count + jnp.arange(count, dtype=jnp.int32)
-    inside = (positions[:, None] >= starts[None, :]) & (
-        positions[:, None] < (starts + frame_tokens)[None, :]
-    )
-    return jnp.pad(inside.astype(BF16), ((0, 0), (0, HD - FRAMES)))
-
-
-def allowed_frames(span_first, span_count, block, own_rows, sub_heads):
-    first = lax.dynamic_slice_in_dim(span_first, block * own_rows, own_rows)[:, None]
-    end = jnp.minimum(
-        first + lax.dynamic_slice_in_dim(span_count, block * own_rows, own_rows)[:, None], FRAMES
-    )
-    ids = jnp.arange(HD, dtype=jnp.int32)[None, :]
-    blocked = jnp.where((ids >= FRAMES) | ((ids >= first) & (ids < end)), 0.0, MASKED)
-    wide = jnp.broadcast_to(blocked.astype(BF16)[:, None, :], (own_rows, sub_heads, HD))
-    return wide.reshape(own_rows * sub_heads, HD)
 
 
 def body(
@@ -371,16 +421,15 @@
 ):
     own_rows, sub_heads, width = queries.shape
     local_heads = width // HD
-    count = projected.shape[0]
     chunk_heads = 2 if local_heads % 2 == 0 else 1
     chunks = local_heads // chunk_heads
     section_count = lax.axis_size("section")
     block_count = lax.axis_size("blk")
-    section = lax.axis_index("section")
-    block = lax.axis_index("blk")
     bits = block_count.bit_length() - 1
-    near, far = 1, 1 << (bits - 1)
-    middle = [1 << bit for bit in range(1, bits - 1)]
+    far = 1 << (bits - 1)
+    lower = [1 << bit for bit in range(bits - 1)]
+    near = [lower[(c + 1) % 2] for c in range(chunks)]
+    middle = [[bit for bit in lower if bit != near[c]] for c in range(chunks)]
 
     def across(x, bit):
         return lax.ppermute(x, "blk", [(i, i ^ bit) for i in range(block_count)])
@@ -399,29 +448,9 @@
     far_queries, near_queries, near_far_queries = [], [], []
     for c in range(chunks):
         far_queries.append(across(own_queries[c], far))
-        near_queries.append(across(own_queries[c], near))
+        near_queries.append(across(own_queries[c], near[c]))
     for c in range(chunks):
-        near_far_queries.append(across(far_queries[c], near))
-
-    starts = frame_starts(frame_tokens)
-    source_bits = [0]
-    for bit in middle:
-        source_bits = source_bits + [other ^ bit for other in source_bits]
-    places = [(s, other) for other in source_bits for s in range(section_count)]
-    frames = jnp.stack(
-        [
-            source_frames(
-                starts,
-                frame_tokens,
-                lax.rem(section + section_count - s, section_count) * block_count + (block ^ other),
-                count,
-            )
-            for s, other in places
-        ]
-    )
-
-    def mask(other):
-        return allowed_frames(span_first, span_count, block ^ other, own_rows, sub_heads)
+        near_far_queries.append(across(far_queries[c], near[c]))
 
     gain = key_gain.reshape(1, HD)
 
@@ -431,8 +460,10 @@
         own, held = project(
             projected, key_weight, value_weight, gain, c, chunk_heads, held, chunks > 1 and c == 0
         )
+        if c == chunks - 1:
+            own, frame_tokens = lax.optimization_barrier((own, frame_tokens))
         plane = [own]
-        for bit in middle:
+        for bit in middle[c]:
             plane = plane + [across(part, bit) for part in plane]
         kv_sources = []
         for part in plane:
@@ -441,19 +472,48 @@
                 kv_sources.append(across_section(part))
         received.append(kv_sources)
 
-    got_back = []
+    starts = frame_starts(frame_tokens)
+    places = []
     for c in range(chunks):
-        (corner,) = attend([([near_far_queries[c]], mask(near ^ far), True)], [received[c]], frames)
-        got_corner = across(corner, near)
-        far_side, near_side = attend(
-            [([far_queries[c]], mask(far), False), ([near_queries[c]], mask(near), True)],
-            [received[c]],
-            frames,
-        )
-        got_near = across(near_side, near)
-        send = merge(got_corner, far_side, rows)
-        got_back.append((got_near, across(send, far)))
-    (home,) = attend([(own_queries, mask(0), False)], received, frames)
+        source_bits = [0]
+        for bit in middle[c]:
+            source_bits = source_bits + [other ^ bit for other in source_bits]
+        places.append([(other, s) for other in source_bits for s in range(section_count)])
+    edges = jnp.pad(jnp.stack([starts, starts + frame_tokens]), ((0, 0), (0, HD - FRAMES)))
+    spans = [span_first.reshape(-1, own_rows), span_count.reshape(-1, own_rows)]
+
+    homes, got_home, got_back = [], [], []
+    for c in range(chunks):
+        every = tuple(range(chunk_heads))
+        pieces = [(head,) for head in every] if c == chunks - 1 else [every]
+        tables = None
+        got_corner = []
+        for heads in pieces:
+            corner, *built = attend(
+                [(near_far_queries[c], near[c] ^ far, True)],
+                spans,
+                tables,
+                heads,
+                None if tables else received[c],
+                edges,
+                () if tables else places[c],
+            )
+            tables = tables or built
+            got_corner.append(across(corner, near[c]))
+        far_group = (far_queries[c], far, False)
+        near_group = (near_queries[c], near[c], True)
+        for index, heads in enumerate(pieces):
+            both = len(pieces) == 1
+            far_side, *near_sides = attend(
+                [far_group, near_group] if both else [far_group], spans, tables, heads
+            )
+            send = merge(got_corner[index], far_side, rows)
+            got_back.append(across(send, far))
+        if not near_sides:
+            near_sides = attend([near_group], spans, tables, every)
+        got_home.append(across(near_sides[0], near[c]))
+        homes += attend([(own_queries[c], 0, False)], spans, tables, every)
+    home = gather_home(homes, got_home, rows)
     return finish(home, got_back, rows, queries.shape)
 
 

time: 109 us -> 110 us (level)
  local copies, waits for them, and re-layouts: 0.64 us -> 9.29 us
  waiting for transfers between devices: 40.9 us -> 36.7 us
  starting transfers between devices: 23.3 us -> 21.2 us
    unnamed x12 -> x16, local copies, waits for them, and re-layouts: 0.04 us -> 7.32 us
    ppermute x14 -> x16, waiting for transfers between devices: 40.9 us -> 36.7 us  [across(): return lax.ppermute(x, 'blk', [(i, i ^ bit) for i in range(block_count)])]
    ppermute x14 -> x16, starting transfers between devices: 23.2 us -> 20.5 us  [across(): return lax.ppermute(x, 'blk', [(i, i ^ bit) for i in range(block_count)])]
    pallas_call x2, Pallas kernels: 15 us -> 13.5 us  [project(): pl.pallas_call(functools.partial(project_kernel, steps, heads, chunk, fet...]
    pallas_call x6 -> x11, Pallas kernels: 27 us -> 28.3 us  [the longest x9 26.2 us: attend(): pl.pallas_call(functools.partial(attend_kernel, tuple((other for _, other...]
  transfers between devices with their start and end apart: 18 -> 20, of which waited for: 7 -> 4; matrix products, arithmetic and copies ran while one was open for 1% -> 2% of each run, Pallas kernels for 24% -> 31%
where the time goes in v2:
time: 110 us
  Pallas kernels  42.7 us (39%)
  waiting for transfers between devices  36.7 us (33%)
  starting transfers between devices  21.2 us (19%)
  local copies, waits for them, and re-layouts  9.29 us (8%)
    ppermute x16, waiting for transfers between devices, across(): return lax.ppermute(x, 'blk', [(i, i ^ bit) for i in range(block_count)])  36.7 us
    pallas_call x9, Pallas kernels, attend(): pl.pallas_call(functools.partial(attend_kernel, tuple((other for _, other...  26.2 us
    ppermute x16, starting transfers between devices, across(): return lax.ppermute(x, 'blk', [(i, i ^ bit) for i in range(block_count)])  20.5 us
    pallas_call x2, Pallas kernels, project(): pl.pallas_call(functools.partial(project_kernel, steps, heads, chunk, fet...  13.5 us
    unnamed x16, local copies, waits for them, and re-layouts  7.32 us
  transfers between devices with their start and end apart: 20, of which 4 were waited for; matrix products, arithmetic and copies ran while one was open for 2% of the time, Pallas kernels for 31%

profile of v2, /device:TPU:0, one launch (start us, length us, event | category | flops | bytes accessed | tf_op | source)
XLA Modules:
  0.0 110.0 jit_solution(2260553024314733230)
XLA Ops:
  0.7 7.0 %shard_map.82 = (bf16[2,512,256]{2,1,0:T(8,128)(2,1)S(1)}, bf16[512,8192]{1,0:T(8,128)(2,1)S(1)}) custom-call(bf16[512,8192]{1,0:T(8,128)(2,1)} %refs_0_.1, bf16[8192,512]{1,0:T(8,128)(2,1)} %refs_1_.3, bf16[8192,512]{1,0:T(8,128)(2,1)} %refs_2_.3, f32[1,128]{1,0:T(1,128)S(1)} %bitcast.24), custom_call_target="tpu_custom_call" | custom-call | flops 4294967296 | bytes 16777216 | tf_op jit(solution)/shard_map/pallas_call | solution.py:78
  7.7 3.3 %copy-done = bf16[512,8192]{1,0:T(8,128)(2,1)} copy-done((bf16[512,8192]{1,0:T(8,128)(2,1)}, bf16[512,8192]{1,0:T(8,128)(2,1)S(1)}, u32[]{:S(2)}) %copy-start) | copy-done | bytes 8388632
  10.9 3.0 %collective-permute-start.3 = (bf16[2,512,256]{2,1,0:T(8,128)(2,1)S(1)}, bf16[2,512,256]{2,1,0:T(8,128)(2,1)S(1)}, u32[]{:S(2)}, u32[]{:S(2)}) collective-permute-start(bf16[2,512,256]{2,1,0:T(8,128)(2,1)S(1)} %get-tuple-element.17.refs_3_), channel_id=1, source_target_pairs={{0,2},{2,0},{4,6},{6,4},{8,10},{10,8},{12,14},{14,12},{1,3},{3,1},... | collective-permute-start | bytes 1572872 | tf_op jit(solution)/shard_map/ppermute | solution.py:435
  14.9 2.7 %collective-permute-start = (bf16[512,256]{1,0:T(8,128)(2,1)S(1)}, bf16[512,256]{1,0:T(8,128)(2,1)S(1)}, u32[]{:S(2)}, u32[]{:S(2)}) collective-permute-start(bf16[512,256]{1,0:T(8,128)(2,1)S(1)} %reshape.16.refs_0_), channel_id=1, source_target_pairs={{0,8},{2,10},{4,12},{6,14},{8,0},{10,2},{12,4},{14,6},{1,9},{3,11}... | collective-permute-start | bytes 786440 | tf_op jit(solution)/shard_map/ppermute | solution.py:435
  17.5 3.4 %copy-done.1 = bf16[512,8192]{1,0:T(8,128)(2,1)S(1)} copy-done((bf16[512,8192]{1,0:T(8,128)(2,1)S(1)}, bf16[512,8192]{1,0:T(8,128)(2,1)}, u32[]{:S(2)}) %copy-start.1) | copy-done | bytes 8388632
  20.9 6.5 %shard_map.83.refs_3_ = bf16[2,512,256]{2,1,0:T(8,128)(2,1)S(1)} custom-call(bf16[512,8192]{1,0:T(8,128)(2,1)S(1)} %copy-done.1, bf16[8192,512]{1,0:T(8,128)(2,1)} %refs_1_.3, bf16[8192,512]{1,0:T(8,128)(2,1)} %refs_2_.3, f32[1,128]{1,0:T(1,128)S(1)} %bitcast.25), custom_call_target="tpu_custom_call" | custom-call | flops 4294967296 | bytes 8388608 | tf_op jit(solution)/shard_map/pallas_call | solution.py:78
  27.5 1.6 %collective-permute-start.8 = (bf16[2,512,256]{2,1,0:T(8,128)(2,1)S(1)}, bf16[2,512,256]{2,1,0:T(8,128)(2,1)S(1)}, u32[]{:S(2)}, u32[]{:S(2)}) collective-permute-start(bf16[2,512,256]{2,1,0:T(8,128)(2,1)S(1)} %shard_map.83.refs_3_), channel_id=1, source_target_pairs={{0,4},{2,6},{4,0},{6,2},{8,12},{10,14},{12,8},{14,10},{1,5},{3,7},... | collective-permute-start | bytes 1572872 | tf_op jit(solution)/shard_map/ppermute | solution.py:435
  31.6 15.4 %collective-permute-done.5.refs_0_ = bf16[512,256]{1,0:T(8,128)(2,1)S(1)} collective-permute-done((bf16[512,256]{1,0:T(8,128)(2,1)S(1)}, bf16[512,256]{1,0:T(8,128)(2,1)S(1)}, u32[]{:S(2)}, u32[]{:S(2)}) %collective-permute-start.5) | collective-permute-done | bytes 262176 | tf_op jit(solution)/shard_map/ppermute | solution.py:435
  48.3 5.3 %collective-permute-done.1.refs_0_ = bf16[512,256]{1,0:T(8,128)(2,1)S(1)} collective-permute-done((bf16[512,256]{1,0:T(8,128)(2,1)S(1)}, bf16[512,256]{1,0:T(8,128)(2,1)S(1)}, u32[]{:S(2)}, u32[]{:S(2)}) %collective-permute-start.1) | collective-permute-done | bytes 262176 | tf_op jit(solution)/shard_map/ppermute | solution.py:435
  54.1 1.6 %collective-permute-start.6 = (bf16[512,256]{1,0:T(8,128)(2,1)S(1)}, bf16[512,256]{1,0:T(8,128)(2,1)S(1)}, u32[]{:S(2)}, u32[]{:S(2)}) collective-permute-start(bf16[512,256]{1,0:T(8,128)(2,1)S(1)} %collective-permute-done.5.refs_0_), channel_id=1, source_target_pairs={{0,2},{2,0},{4,6},{6,4},{8,10},{10,8},{12,14},{14,12},{1,3},{3,1},... | collective-permute-start | bytes 786440 | tf_op jit(solution)/shard_map/ppermute | solution.py:435
  55.8 4.5 %shard_map.84 = (bf16[2,528,128]{2,1,0:T(8,128)(2,1)S(1)}, bf16[2,2048,256]{2,1,0:T(8,128)(2,1)S(1)}, bf16[2,2048,256]{2,1,0:T(8,128)(2,1)S(1)}) custom-call(bf16[512,256]{1,0:T(8,128)(2,1)S(1)} %collective-permute-done.1.refs_0_, s32[8,128]{1,0:T(8,128)S(1)} %bitcast.6, s32[8,128]{1,0:T(8,128)S(1)} %bitcast.15, ...), custom_call_target="tpu_custom_call" | custom-call | flops 2147483648 | bytes 2621440 | tf_op jit(solution)/shard_map/pallas_call | solution.py:294
  60.3 6.1 %shard_map.88 = (f32[2,520,128]{2,1,0:T(8,128)S(1)}, bf16[2,528,128]{2,1,0:T(8,128)(2,1)S(1)}) custom-call(bf16[512,256]{1,0:T(8,128)(2,1)S(1)} %collective-permute-done.refs_0_, bf16[512,256]{1,0:T(8,128)(2,1)S(1)} %collective-permute-done.10.refs_1_, s32[8,128]{1,0:T(8,128)S(1)} %bitcast.7, s32[8,128]{1,0:T(8,128)S(1)} %bitcast.16, ...), custom_call_target="tpu_custom_call" | custom-call | flops 4294967296 | bytes 3145728 | tf_op jit(solution)/shard_map/pallas_call | solution.py:294
  66.5 1.6 %collective-permute-start.11 = (bf16[2,528,128]{2,1,0:T(8,128)(2,1)S(1)}, bf16[2,528,128]{2,1,0:T(8,128)(2,1)S(1)}, u32[]{:S(2)}, u32[]{:S(2)}) collective-permute-start(bf16[2,528,128]{2,1,0:T(8,128)(2,1)S(1)} %get-tuple-element.25), channel_id=1, source_target_pairs={{0,4},{2,6},{4,0},{6,2},{8,12},{10,14},{12,8},{14,10},{1,5},{3,7},... | collective-permute-start | bytes 811016 | tf_op jit(solution)/shard_map/ppermute | solution.py:435
  68.6 2.0 %shard_map.86 = (bf16[1,528,128]{2,1,0:T(8,128)(2,1)S(1)}, bf16[2,2048,256]{2,1,0:T(8,128)(2,1)S(1)}, bf16[2,2048,256]{2,1,0:T(8,128)(2,1)S(1)}) custom-call(bf16[512,256]{1,0:T(8,128)(2,1)S(1)} %collective-permute-done.6.refs_0_, s32[8,128]{1,0:T(8,128)S(1)} %bitcast.8, s32[8,128]{1,0:T(8,128)S(1)} %bitcast.17, bf16[2,512,256]{2,1,0:T(8,128)(2,1)S(1)} %shard_map.83.refs_3_, ...), custom_call_target="tpu_custom_call" | custom-call | flops 1073741824 | bytes 1310720 | tf_op jit(solution)/shard_map/pallas_call | solution.py:294
  71.2 1.5 %shard_map.93 = bf16[1,528,128]{2,1,0:T(8,128)(2,1)S(1)} custom-call(bf16[512,256]{1,0:T(8,128)(2,1)S(1)} %collective-permute-done.6.refs_0_, s32[8,128]{1,0:T(8,128)S(1)} %bitcast.9, s32[8,128]{1,0:T(8,128)S(1)} %bitcast.18, bf16[2,2048,256]{2,1,0:T(8,128)(2,1)S(1)} %get-tuple-element.23.refs_3_, bf16[2,2048,256]{2,1,0:T(8,128)(2,1)S(1)} %get-tuple-element.24.refs_4_), custom_call_target="tpu_custom_call" | custom-call | flops 1073741824 | bytes 1310720 | tf_op jit(solution)/shard_map/pallas_call | solution.py:294
  72.7 1.6 %collective-permute-start.18 = (bf16[1,528,128]{2,1,0:T(8,128)(2,1)S(1)}, bf16[1,528,128]{2,1,0:T(8,128)(2,1)S(1)}, u32[]{:S(2)}, u32[]{:S(2)}) collective-permute-start(bf16[1,528,128]{2,1,0:T(8,128)(2,1)S(1)} %shard_map.93), channel_id=1, source_target_pairs={{0,2},{2,0},{4,6},{6,4},{8,10},{10,8},{12,14},{14,12},{1,3},{3,1},... | collective-permute-start | bytes 405512 | tf_op jit(solution)/shard_map/ppermute | solution.py:435
  74.3 2.9 %shard_map.89 = bf16[2,528,128]{2,1,0:T(8,128)(2,1)S(1)} custom-call(bf16[512,256]{1,0:T(8,128)(2,1)S(1)} %collective-permute-done.12.refs_0_, s32[8,128]{1,0:T(8,128)S(1)} %bitcast.10, s32[8,128]{1,0:T(8,128)S(1)} %bitcast.19, bf16[2,2048,256]{2,1,0:T(8,128)(2,1)S(1)} %get-tuple-element.23.refs_3_, bf16[2,2048,256]{2,1,0:T(8,128)(2,1)S(1)} %get-tuple-element.24.refs_4_), custom_call_target="tpu_custom_call" | custom-call | flops 2147483648 | bytes 2621440 | tf_op jit(solution)/shard_map/pallas_call | solution.py:294
  77.7 3.3 %shard_map.85.refs_0_ = f32[2,520,128]{2,1,0:T(8,128)S(1)} custom-call(bf16[512,256]{1,0:T(8,128)(2,1)S(1)} %reshape.16.refs_0_, s32[8,128]{1,0:T(8,128)S(1)} %bitcast.11, s32[8,128]{1,0:T(8,128)S(1)} %bitcast.20, bf16[2,2048,256]{2,1,0:T(8,128)(2,1)S(1)} %get-tuple-element.20.refs_3_.refs_4_, bf16[2,2048,256]{2,1,0:T(8,128)(2,1)S(1)} %get-tuple-element.21.refs_4_.refs_5_), custom_call_target="tpu_custom_call" | custom-call | flops 2147483648 | bytes 2621440 | tf_op jit(solution)/shard_map/pallas_call | solution.py:294
  81.0 1.5 %shard_map.94.own_ref = f32[1,520,128]{2,1,0:T(8,128)S(1)} custom-call(bf16[512,256]{1,0:T(8,128)(2,1)S(1)} %collective-permute-done.5.refs_0_, s32[8,128]{1,0:T(8,128)S(1)} %bitcast.12, s32[8,128]{1,0:T(8,128)S(1)} %bitcast.21, bf16[2,2048,256]{2,1,0:T(8,128)(2,1)S(1)} %get-tuple-element.23.refs_3_, bf16[2,2048,256]{2,1,0:T(8,128)(2,1)S(1)} %get-tuple-element.24.refs_4_), custom_call_target="tpu_custom_call" | custom-call | flops 1073741824 | bytes 1310720 | tf_op jit(solution)/shard_map/pallas_call | solution.py:294
  84.0 1.5 %shard_map.91.own_ref = f32[1,520,128]{2,1,0:T(8,128)S(1)} custom-call(bf16[512,256]{1,0:T(8,128)(2,1)S(1)} %collective-permute-done.5.refs_0_, s32[8,128]{1,0:T(8,128)S(1)} %bitcast.13, s32[8,128]{1,0:T(8,128)S(1)} %bitcast.22, bf16[2,2048,256]{2,1,0:T(8,128)(2,1)S(1)} %get-tuple-element.23.refs_3_, bf16[2,2048,256]{2,1,0:T(8,128)(2,1)S(1)} %get-tuple-element.24.refs_4_), custom_call_target="tpu_custom_call" | custom-call | flops 1073741824 | bytes 1310720 | tf_op jit(solution)/shard_map/pallas_call | solution.py:294
  85.8 2.0 %collective-permute-start.17 = (bf16[1,528,128]{2,1,0:T(8,128)(2,1)S(1)}, bf16[1,528,128]{2,1,0:T(8,128)(2,1)S(1)}, u32[]{:S(2)}, u32[]{:S(2)}) collective-permute-start(bf16[1,528,128]{2,1,0:T(8,128)(2,1)S(1)} %shard_map.92), channel_id=1, source_target_pairs={{0,8},{2,10},{4,12},{6,14},{8,0},{10,2},{12,4},{14,6},{1,9},{3,11}... | collective-permute-start | bytes 405512 | tf_op jit(solution)/shard_map/ppermute | solution.py:435
  89.1 2.9 %shard_map.87.refs_1_ = f32[2,520,128]{2,1,0:T(8,128)S(1)} custom-call(bf16[512,256]{1,0:T(8,128)(2,1)S(1)} %reshape.20.refs_0_, s32[8,128]{1,0:T(8,128)S(1)} %bitcast.14, s32[8,128]{1,0:T(8,128)S(1)} %bitcast.23, bf16[2,2048,256]{2,1,0:T(8,128)(2,1)S(1)} %get-tuple-element.23.refs_3_, bf16[2,2048,256]{2,1,0:T(8,128)(2,1)S(1)} %get-tuple-element.24.refs_4_), custom_call_target="tpu_custom_call" | custom-call | flops 2147483648 | bytes 2621440 | tf_op jit(solution)/shard_map/pallas_call | solution.py:294
  92.6 14.2 %collective-permute-done.17.refs_1_ = bf16[1,528,128]{2,1,0:T(8,128)(2,1)S(1)} collective-permute-done((bf16[1,528,128]{2,1,0:T(8,128)(2,1)S(1)}, bf16[1,528,128]{2,1,0:T(8,128)(2,1)S(1)}, u32[]{:S(2)}, u32[]{:S(2)}) %collective-permute-start.17) | collective-permute-done | bytes 135200 | tf_op jit(solution)/shard_map/ppermute | solution.py:435
  106.8 1.8 %collective-permute-done.19.refs_2_ = bf16[1,528,128]{2,1,0:T(8,128)(2,1)S(1)} collective-permute-done((bf16[1,528,128]{2,1,0:T(8,128)(2,1)S(1)}, bf16[1,528,128]{2,1,0:T(8,128)(2,1)S(1)}, u32[]{:S(2)}, u32[]{:S(2)}) %collective-permute-start.19) | collective-permute-done | bytes 135200 | tf_op jit(solution)/shard_map/ppermute | solution.py:435
  (55 shorter events, 12.8 us)
Async XLA Ops:
  0.7 13.3 %copy-start.6 = (bf16[128,4,512]{2,1,0:T(4,128)(2,1)S(1)}, bf16[128,4,512]{2,1,0:T(4,128)(2,1)}, u32[]{:S(2)}) copy-start(bf16[128,4,512]{2,1,0:T(4,128)(2,1)} %param.12) | copy-start | bytes 1572868
  0.7 16.9 %copy-start.5 = (f32[128]{0:T(128)S(1)}, f32[128]{0:T(128)}, u32[]{:S(2)}) copy-start(f32[128]{0:T(128)} %param.11) | copy-start | bytes 1540
  10.9 18.2 %collective-permute-start.3 = (bf16[2,512,256]{2,1,0:T(8,128)(2,1)S(1)}, bf16[2,512,256]{2,1,0:T(8,128)(2,1)S(1)}, u32[]{:S(2)}, u32[]{:S(2)}) collective-permute-start(bf16[2,512,256]{2,1,0:T(8,128)(2,1)S(1)} %get-tuple-element.17.refs_3_), channel_id=1, source_target_pairs={{0,2},{2,0},{4,6},{6,4},{8,10},{10,8},{12,14},{14,12},{1,3},{3,1},... | collective-permute-start | bytes 1572872 | tf_op jit(solution)/shard_map/ppermute | solution.py:435
  14.9 16.2 %collective-permute-start = (bf16[512,256]{1,0:T(8,128)(2,1)S(1)}, bf16[512,256]{1,0:T(8,128)(2,1)S(1)}, u32[]{:S(2)}, u32[]{:S(2)}) collective-permute-start(bf16[512,256]{1,0:T(8,128)(2,1)S(1)} %reshape.16.refs_0_), channel_id=1, source_target_pairs={{0,8},{2,10},{4,12},{6,14},{8,0},{10,2},{12,4},{14,6},{1,9},{3,11}... | collective-permute-start | bytes 786440 | tf_op jit(solution)/shard_map/ppermute | solution.py:435
  20.9 34.9 %copy-start.2 = (s32[1024]{0:T(1024)S(1)}, s32[1024]{0:T(1024)}, u32[]{:S(2)}) copy-start(s32[1024]{0:T(1024)} %param.14) | copy-start | bytes 12292
  20.9 34.9 %copy-start.3 = (s32[1024]{0:T(1024)S(1)}, s32[1024]{0:T(1024)}, u32[]{:S(2)}) copy-start(s32[1024]{0:T(1024)} %param.15) | copy-start | bytes 12292
  27.5 26.6 %collective-permute-start.8 = (bf16[2,512,256]{2,1,0:T(8,128)(2,1)S(1)}, bf16[2,512,256]{2,1,0:T(8,128)(2,1)S(1)}, u32[]{:S(2)}, u32[]{:S(2)}) collective-permute-start(bf16[2,512,256]{2,1,0:T(8,128)(2,1)S(1)} %shard_map.83.refs_3_), channel_id=1, source_target_pairs={{0,4},{2,6},{4,0},{6,2},{8,12},{10,14},{12,8},{14,10},{1,5},{3,7},... | collective-permute-start | bytes 1572872 | tf_op jit(solution)/shard_map/ppermute | solution.py:435
  29.1 25.0 %collective-permute-start.2 = (bf16[2,512,256]{2,1,0:T(8,128)(2,1)S(1)}, bf16[2,512,256]{2,1,0:T(8,128)(2,1)S(1)}, u32[]{:S(2)}, u32[]{:S(2)}) collective-permute-start(bf16[2,512,256]{2,1,0:T(8,128)(2,1)S(1)} %get-tuple-element.17.refs_3_), channel_id=1, source_target_pairs={{0,16},{16,0},{1,17},{17,1},{2,18},{18,2},{3,19},{19,3},{4,20},{20... | collective-permute-start | bytes 1572872 | tf_op jit(solution)/shard_map/ppermute | solution.py:438
  29.1 26.6 %collective-permute-start.4 = (bf16[2,512,256]{2,1,0:T(8,128)(2,1)S(1)}, bf16[2,512,256]{2,1,0:T(8,128)(2,1)}, u32[]{:S(2)}, u32[]{:S(2)}) collective-permute-start(bf16[2,512,256]{2,1,0:T(8,128)(2,1)S(1)} %collective-permute-done.3.refs_5_), channel_id=1, source_target_pairs={{0,16},{16,0},{1,17},{17,1},{2,18},{18,2},{3,19},{19,3},{4,20},{20... | collective-permute-start | bytes 1572872 | tf_op jit(solution)/shard_map/ppermute | solution.py:438
  30.6 16.4 %collective-permute-start.5 = (bf16[512,256]{1,0:T(8,128)(2,1)S(1)}, bf16[512,256]{1,0:T(8,128)(2,1)S(1)}, u32[]{:S(2)}, u32[]{:S(2)}) collective-permute-start(bf16[512,256]{1,0:T(8,128)(2,1)S(1)} %reshape.20.refs_0_), channel_id=1, source_target_pairs={{0,8},{2,10},{4,12},{6,14},{8,0},{10,2},{12,4},{14,6},{1,9},{3,11}... | collective-permute-start | bytes 786440 | tf_op jit(solution)/shard_map/ppermute | solution.py:435
  31.1 22.4 %collective-permute-start.1 = (bf16[512,256]{1,0:T(8,128)(2,1)S(1)}, bf16[512,256]{1,0:T(8,128)(2,1)S(1)}, u32[]{:S(2)}, u32[]{:S(2)}) collective-permute-start(bf16[512,256]{1,0:T(8,128)(2,1)S(1)} %collective-permute-done.refs_0_), channel_id=1, source_target_pairs={{0,4},{2,6},{4,0},{6,2},{8,12},{10,14},{12,8},{14,10},{1,5},{3,7},... | collective-permute-start | bytes 786440 | tf_op jit(solution)/shard_map/ppermute | solution.py:435
  47.0 13.3 %collective-permute-start.10 = (bf16[512,256]{1,0:T(8,128)(2,1)S(1)}, bf16[512,256]{1,0:T(8,128)(2,1)S(1)}, u32[]{:S(2)}, u32[]{:S(2)}) collective-permute-start(bf16[512,256]{1,0:T(8,128)(2,1)S(1)} %reshape.16.refs_0_), channel_id=1, source_target_pairs={{0,4},{2,6},{4,0},{6,2},{8,12},{10,14},{12,8},{14,10},{1,5},{3,7},... | collective-permute-start | bytes 786440 | tf_op jit(solution)/shard_map/ppermute | solution.py:435
  53.5 20.7 %collective-permute-start.12 = (bf16[512,256]{1,0:T(8,128)(2,1)S(1)}, bf16[512,256]{1,0:T(8,128)(2,1)S(1)}, u32[]{:S(2)}, u32[]{:S(2)}) collective-permute-start(bf16[512,256]{1,0:T(8,128)(2,1)S(1)} %reshape.20.refs_0_), channel_id=1, source_target_pairs={{0,2},{2,0},{4,6},{6,4},{8,10},{10,8},{12,14},{14,12},{1,3},{3,1},... | collective-permute-start | bytes 786440 | tf_op jit(solution)/shard_map/ppermute | solution.py:435
  54.1 14.5 %collective-permute-start.7 = (bf16[2,512,256]{2,1,0:T(8,128)(2,1)S(1)}, bf16[2,512,256]{2,1,0:T(8,128)(2,1)S(1)}, u32[]{:S(2)}, u32[]{:S(2)}) collective-permute-start(bf16[2,512,256]{2,1,0:T(8,128)(2,1)S(1)} %shard_map.83.refs_3_), channel_id=1, source_target_pairs={{0,16},{16,0},{1,17},{17,1},{2,18},{18,2},{3,19},{19,3},{4,20},{20... | collective-permute-start | bytes 1572872 | tf_op jit(solution)/shard_map/ppermute | solution.py:438
  54.1 14.0 %collective-permute-start.6 = (bf16[512,256]{1,0:T(8,128)(2,1)S(1)}, bf16[512,256]{1,0:T(8,128)(2,1)S(1)}, u32[]{:S(2)}, u32[]{:S(2)}) collective-permute-start(bf16[512,256]{1,0:T(8,128)(2,1)S(1)} %collective-permute-done.5.refs_0_), channel_id=1, source_target_pairs={{0,2},{2,0},{4,6},{6,4},{8,10},{10,8},{12,14},{14,12},{1,3},{3,1},... | collective-permute-start | bytes 786440 | tf_op jit(solution)/shard_map/ppermute | solution.py:435
  55.7 12.9 %collective-permute-start.9 = (bf16[2,512,256]{2,1,0:T(8,128)(2,1)S(1)}, bf16[2,512,256]{2,1,0:T(8,128)(2,1)S(1)}, u32[]{:S(2)}, u32[]{:S(2)}) collective-permute-start(bf16[2,512,256]{2,1,0:T(8,128)(2,1)S(1)} %collective-permute-done.8.refs_5_), channel_id=1, source_target_pairs={{0,16},{16,0},{1,17},{17,1},{2,18},{18,2},{3,19},{19,3},{4,20},{20... | collective-permute-start | bytes 1572872 | tf_op jit(solution)/shard_map/ppermute | solution.py:438
  66.5 25.5 %collective-permute-start.11 = (bf16[2,528,128]{2,1,0:T(8,128)(2,1)S(1)}, bf16[2,528,128]{2,1,0:T(8,128)(2,1)S(1)}, u32[]{:S(2)}, u32[]{:S(2)}) collective-permute-start(bf16[2,528,128]{2,1,0:T(8,128)(2,1)S(1)} %get-tuple-element.25), channel_id=1, source_target_pairs={{0,4},{2,6},{4,0},{6,2},{8,12},{10,14},{12,8},{14,10},{1,5},{3,7},... | collective-permute-start | bytes 811016 | tf_op jit(solution)/shard_map/ppermute | solution.py:435
  68.1 14.5 %collective-permute-start.14 = (bf16[2,528,128]{2,1,0:T(8,128)(2,1)S(1)}, bf16[2,528,128]{2,1,0:T(8,128)(2,1)S(1)}, u32[]{:S(2)}, u32[]{:S(2)}) collective-permute-start(bf16[2,528,128]{2,1,0:T(8,128)(2,1)S(1)} %get-tuple-element.26), channel_id=1, source_target_pairs={{0,4},{2,6},{4,0},{6,2},{8,12},{10,14},{12,8},{14,10},{1,5},{3,7},... | collective-permute-start | bytes 811016 | tf_op jit(solution)/shard_map/ppermute | solution.py:435
  70.6 14.9 %collective-permute-start.16 = (bf16[1,528,128]{2,1,0:T(8,128)(2,1)S(1)}, bf16[1,528,128]{2,1,0:T(8,128)(2,1)S(1)}, u32[]{:S(2)}, u32[]{:S(2)}) collective-permute-start(bf16[1,528,128]{2,1,0:T(8,128)(2,1)S(1)} %get-tuple-element.28), channel_id=1, source_target_pairs={{0,2},{2,0},{4,6},{6,4},{8,10},{10,8},{12,14},{14,12},{1,3},{3,1},... | collective-permute-start | bytes 405512 | tf_op jit(solution)/shard_map/ppermute | solution.py:435
  72.7 15.1 %collective-permute-start.18 = (bf16[1,528,128]{2,1,0:T(8,128)(2,1)S(1)}, bf16[1,528,128]{2,1,0:T(8,128)(2,1)S(1)}, u32[]{:S(2)}, u32[]{:S(2)}) collective-permute-start(bf16[1,528,128]{2,1,0:T(8,128)(2,1)S(1)} %shard_map.93), channel_id=1, source_target_pairs={{0,2},{2,0},{4,6},{6,4},{8,10},{10,8},{12,14},{14,12},{1,3},{3,1},... | collective-permute-start | bytes 405512 | tf_op jit(solution)/shard_map/ppermute | solution.py:435
  77.2 14.8 %collective-permute-start.13 = (bf16[2,528,128]{2,1,0:T(8,128)(2,1)S(1)}, bf16[2,528,128]{2,1,0:T(8,128)(2,1)S(1)}, u32[]{:S(2)}, u32[]{:S(2)}) collective-permute-start(bf16[2,528,128]{2,1,0:T(8,128)(2,1)S(1)} %shard_map.89), channel_id=1, source_target_pairs={{0,2},{2,0},{4,6},{6,4},{8,10},{10,8},{12,14},{14,12},{1,3},{3,1},... | collective-permute-start | bytes 811016 | tf_op jit(solution)/shard_map/ppermute | solution.py:435
  82.9 25.7 %collective-permute-start.15 = (bf16[2,528,128]{2,1,0:T(8,128)(2,1)S(1)}, bf16[2,528,128]{2,1,0:T(8,128)(2,1)S(1)}, u32[]{:S(2)}, u32[]{:S(2)}) collective-permute-start(bf16[2,528,128]{2,1,0:T(8,128)(2,1)S(1)} %shard_map.90), channel_id=1, source_target_pairs={{0,8},{2,10},{4,12},{6,14},{8,0},{10,2},{12,4},{14,6},{1,9},{3,11}... | collective-permute-start | bytes 811016 | tf_op jit(solution)/shard_map/ppermute | solution.py:435
  85.8 21.0 %collective-permute-start.17 = (bf16[1,528,128]{2,1,0:T(8,128)(2,1)S(1)}, bf16[1,528,128]{2,1,0:T(8,128)(2,1)S(1)}, u32[]{:S(2)}, u32[]{:S(2)}) collective-permute-start(bf16[1,528,128]{2,1,0:T(8,128)(2,1)S(1)} %shard_map.92), channel_id=1, source_target_pairs={{0,8},{2,10},{4,12},{6,14},{8,0},{10,2},{12,4},{14,6},{1,9},{3,11}... | collective-permute-start | bytes 405512 | tf_op jit(solution)/shard_map/ppermute | solution.py:435
  88.0 20.6 %collective-permute-start.19 = (bf16[1,528,128]{2,1,0:T(8,128)(2,1)S(1)}, bf16[1,528,128]{2,1,0:T(8,128)(2,1)S(1)}, u32[]{:S(2)}, u32[]{:S(2)}) collective-permute-start(bf16[1,528,128]{2,1,0:T(8,128)(2,1)S(1)} %shard_map.95), channel_id=1, source_target_pairs={{0,8},{2,10},{4,12},{6,14},{8,0},{10,2},{12,4},{14,6},{1,9},{3,11}... | collective-permute-start | bytes 405512 | tf_op jit(solution)/shard_map/ppermute | solution.py:435
  (4 other events, 17.4 us)

commit v3 on v2

--- a/solution.py
+++ b/solution.py
@@ -380,7 +380,7 @@
             flops=8 * slots * rows * HD, bytes_accessed=8 * slots * rows * HD, transcendentals=0
         ),
         compiler_params=pltpu.CompilerParams(vmem_limit_bytes=32 * MIB),
-        name="gather_home",
+        name="gather",
     )(*own, *received)
 
 
@@ -445,6 +445,7 @@
         queries[:, :, c * chunk_width : (c + 1) * chunk_width].reshape(rows, chunk_width)
         for c in range(chunks)
     ]
+    own_queries = lax.optimization_barrier(own_queries)
     far_queries, near_queries, near_far_queries = [], [], []
     for c in range(chunks):
         far_queries.append(across(own_queries[c], far))
@@ -513,8 +514,8 @@
             near_sides = attend([near_group], spans, tables, every)
         got_home.append(across(near_sides[0], near[c]))
         homes += attend([(own_queries[c], 0, False)], spans, tables, every)
-    home = gather_home(homes, got_home, rows)
-    return finish(home, got_back, rows, queries.shape)
+    home = gather_home(homes, got_back, rows)
+    return finish(home, got_home, rows, queries.shape)
 
 
 def solution(mesh):

time: 110 us -> 110 us (level)
  local copies, waits for them, and re-layouts: 9.29 us -> 7.65 us
  transfers between devices with their start and end apart: 20 -> 20, of which waited for: 4 -> 4; matrix products, arithmetic and copies ran while one was open for 2% -> 0% of each run, Pallas kernels for 31% -> 31%
where the time goes in v3:
time: 110 us
  Pallas kernels  42.1 us (38%)
  waiting for transfers between devices  37.5 us (34%)
  starting transfers between devices  22.1 us (20%)
  local copies, waits for them, and re-layouts  7.65 us (7%)
    ppermute x16, waiting for transfers between devices, across(): return lax.ppermute(x, 'blk', [(i, i ^ bit) for i in range(block_count)])  37.5 us
    pallas_call x9, Pallas kernels, attend(): pl.pallas_call(functools.partial(attend_kernel, tuple((other for _, other...  25.6 us
    ppermute x16, starting transfers between devices, across(): return lax.ppermute(x, 'blk', [(i, i ^ bit) for i in range(block_count)])  21.5 us
    pallas_call x2, Pallas kernels, project(): pl.pallas_call(functools.partial(project_kernel, steps, heads, chunk, fet...  13.5 us
    unnamed x16, local copies, waits for them, and re-layouts  7.32 us
  transfers between devices with their start and end apart: 20, of which 4 were waited for; matrix products, arithmetic and copies ran while one was open for 0% of the time, Pallas kernels for 31%

profile of v3, /device:TPU:0, one launch (start us, length us, event | category | flops | bytes accessed | tf_op | source)
XLA Modules:
  0.0 109.6 jit_solution(10504182447062086803)
XLA Ops:
  0.7 7.0 %shard_map.82 = (bf16[2,512,256]{2,1,0:T(8,128)(2,1)S(1)}, bf16[512,8192]{1,0:T(8,128)(2,1)S(1)}) custom-call(bf16[512,8192]{1,0:T(8,128)(2,1)} %refs_0_.1, bf16[8192,512]{1,0:T(8,128)(2,1)} %refs_1_.3, bf16[8192,512]{1,0:T(8,128)(2,1)} %refs_2_.3, f32[1,128]{1,0:T(1,128)S(1)} %bitcast.24), custom_call_target="tpu_custom_call" | custom-call | flops 4294967296 | bytes 16777216 | tf_op jit(solution)/shard_map/pallas_call | solution.py:78
  7.7 3.3 %copy-done = bf16[512,8192]{1,0:T(8,128)(2,1)} copy-done((bf16[512,8192]{1,0:T(8,128)(2,1)}, bf16[512,8192]{1,0:T(8,128)(2,1)S(1)}, u32[]{:S(2)}) %copy-start) | copy-done | bytes 8388632
  10.9 3.0 %collective-permute-start.3 = (bf16[2,512,256]{2,1,0:T(8,128)(2,1)S(1)}, bf16[2,512,256]{2,1,0:T(8,128)(2,1)S(1)}, u32[]{:S(2)}, u32[]{:S(2)}) collective-permute-start(bf16[2,512,256]{2,1,0:T(8,128)(2,1)S(1)} %get-tuple-element.20.refs_3_), channel_id=1, source_target_pairs={{0,2},{2,0},{4,6},{6,4},{8,10},{10,8},{12,14},{14,12},{1,3},{3,1},... | collective-permute-start | bytes 1572872 | tf_op jit(solution)/shard_map/ppermute | solution.py:435
  14.3 2.7 %collective-permute-start = (bf16[512,256]{1,0:T(8,128)(2,1)S(1)}, bf16[512,256]{1,0:T(8,128)(2,1)S(1)}, u32[]{:S(2)}, u32[]{:S(2)}) collective-permute-start(bf16[512,256]{1,0:T(8,128)(2,1)S(1)} %reshape.16.refs_0_), channel_id=1, source_target_pairs={{0,8},{2,10},{4,12},{6,14},{8,0},{10,2},{12,4},{14,6},{1,9},{3,11}... | collective-permute-start | bytes 786440 | tf_op jit(solution)/shard_map/ppermute | solution.py:435
  16.9 3.4 %copy-done.1 = bf16[512,8192]{1,0:T(8,128)(2,1)S(1)} copy-done((bf16[512,8192]{1,0:T(8,128)(2,1)S(1)}, bf16[512,8192]{1,0:T(8,128)(2,1)}, u32[]{:S(2)}) %copy-start.1) | copy-done | bytes 8388632
  20.3 6.5 %shard_map.83.refs_3_ = bf16[2,512,256]{2,1,0:T(8,128)(2,1)S(1)} custom-call(bf16[512,8192]{1,0:T(8,128)(2,1)S(1)} %copy-done.1, bf16[8192,512]{1,0:T(8,128)(2,1)} %refs_1_.3, bf16[8192,512]{1,0:T(8,128)(2,1)} %refs_2_.3, f32[1,128]{1,0:T(1,128)S(1)} %bitcast.25), custom_call_target="tpu_custom_call" | custom-call | flops 4294967296 | bytes 8388608 | tf_op jit(solution)/shard_map/pallas_call | solution.py:78
  26.8 1.6 %collective-permute-start.8 = (bf16[2,512,256]{2,1,0:T(8,128)(2,1)S(1)}, bf16[2,512,256]{2,1,0:T(8,128)(2,1)S(1)}, u32[]{:S(2)}, u32[]{:S(2)}) collective-permute-start(bf16[2,512,256]{2,1,0:T(8,128)(2,1)S(1)} %shard_map.83.refs_3_), channel_id=1, source_target_pairs={{0,4},{2,6},{4,0},{6,2},{8,12},{10,14},{12,8},{14,10},{1,5},{3,7},... | collective-permute-start | bytes 1572872 | tf_op jit(solution)/shard_map/ppermute | solution.py:435
  30.4 16.0 %collective-permute-done.5.refs_0_ = bf16[512,256]{1,0:T(8,128)(2,1)S(1)} collective-permute-done((bf16[512,256]{1,0:T(8,128)(2,1)S(1)}, bf16[512,256]{1,0:T(8,128)(2,1)S(1)}, u32[]{:S(2)}, u32[]{:S(2)}) %collective-permute-start.5) | collective-permute-done | bytes 262176 | tf_op jit(solution)/shard_map/ppermute | solution.py:435
  47.7 5.3 %collective-permute-done.1.refs_0_ = bf16[512,256]{1,0:T(8,128)(2,1)S(1)} collective-permute-done((bf16[512,256]{1,0:T(8,128)(2,1)S(1)}, bf16[512,256]{1,0:T(8,128)(2,1)S(1)}, u32[]{:S(2)}, u32[]{:S(2)}) %collective-permute-start.1) | collective-permute-done | bytes 262176 | tf_op jit(solution)/shard_map/ppermute | solution.py:435
  53.5 1.6 %collective-permute-start.6 = (bf16[512,256]{1,0:T(8,128)(2,1)S(1)}, bf16[512,256]{1,0:T(8,128)(2,1)S(1)}, u32[]{:S(2)}, u32[]{:S(2)}) collective-permute-start(bf16[512,256]{1,0:T(8,128)(2,1)S(1)} %collective-permute-done.5.refs_0_), channel_id=1, source_target_pairs={{0,2},{2,0},{4,6},{6,4},{8,10},{10,8},{12,14},{14,12},{1,3},{3,1},... | collective-permute-start | bytes 786440 | tf_op jit(solution)/shard_map/ppermute | solution.py:435
  55.2 3.5 %shard_map.84 = (bf16[2,528,128]{2,1,0:T(8,128)(2,1)S(1)}, bf16[2,2048,256]{2,1,0:T(8,128)(2,1)S(1)}, bf16[2,2048,256]{2,1,0:T(8,128)(2,1)S(1)}) custom-call(bf16[512,256]{1,0:T(8,128)(2,1)S(1)} %collective-permute-done.1.refs_0_, s32[8,128]{1,0:T(8,128)S(1)} %bitcast.6, s32[8,128]{1,0:T(8,128)S(1)} %bitcast.15, ...), custom_call_target="tpu_custom_call" | custom-call | flops 2147483648 | bytes 2621440 | tf_op jit(solution)/shard_map/pallas_call | solution.py:294
  58.8 6.5 %shard_map.88 = (f32[2,520,128]{2,1,0:T(8,128)S(1)}, bf16[2,528,128]{2,1,0:T(8,128)(2,1)S(1)}) custom-call(bf16[512,256]{1,0:T(8,128)(2,1)S(1)} %collective-permute-done.refs_0_, bf16[512,256]{1,0:T(8,128)(2,1)S(1)} %collective-permute-done.11.refs_1_, s32[8,128]{1,0:T(8,128)S(1)} %bitcast.7, s32[8,128]{1,0:T(8,128)S(1)} %bitcast.16, ...), custom_call_target="tpu_custom_call" | custom-call | flops 4294967296 | bytes 3145728 | tf_op jit(solution)/shard_map/pallas_call | solution.py:294
  65.3 1.6 %collective-permute-start.17 = (bf16[2,528,128]{2,1,0:T(8,128)(2,1)S(1)}, bf16[2,528,128]{2,1,0:T(8,128)(2,1)S(1)}, u32[]{:S(2)}, u32[]{:S(2)}) collective-permute-start(bf16[2,528,128]{2,1,0:T(8,128)(2,1)S(1)} %get-tuple-element.32), channel_id=1, source_target_pairs={{0,4},{2,6},{4,0},{6,2},{8,12},{10,14},{12,8},{14,10},{1,5},{3,7},... | collective-permute-start | bytes 811016 | tf_op jit(solution)/shard_map/ppermute | solution.py:435
  67.4 2.1 %shard_map.86 = (bf16[1,528,128]{2,1,0:T(8,128)(2,1)S(1)}, bf16[2,2048,256]{2,1,0:T(8,128)(2,1)S(1)}, bf16[2,2048,256]{2,1,0:T(8,128)(2,1)S(1)}) custom-call(bf16[512,256]{1,0:T(8,128)(2,1)S(1)} %collective-permute-done.6.refs_0_, s32[8,128]{1,0:T(8,128)S(1)} %bitcast.8, s32[8,128]{1,0:T(8,128)S(1)} %bitcast.17, bf16[2,512,256]{2,1,0:T(8,128)(2,1)S(1)} %shard_map.83.refs_3_, ...), custom_call_target="tpu_custom_call" | custom-call | flops 1073741824 | bytes 1310720 | tf_op jit(solution)/shard_map/pallas_call | solution.py:294
  70.0 1.5 %shard_map.92 = bf16[1,528,128]{2,1,0:T(8,128)(2,1)S(1)} custom-call(bf16[512,256]{1,0:T(8,128)(2,1)S(1)} %collective-permute-done.6.refs_0_, s32[8,128]{1,0:T(8,128)S(1)} %bitcast.9, s32[8,128]{1,0:T(8,128)S(1)} %bitcast.18, bf16[2,2048,256]{2,1,0:T(8,128)(2,1)S(1)} %get-tuple-element.27.refs_3_, bf16[2,2048,256]{2,1,0:T(8,128)(2,1)S(1)} %get-tuple-element.28.refs_4_), custom_call_target="tpu_custom_call" | custom-call | flops 1073741824 | bytes 1310720 | tf_op jit(solution)/shard_map/pallas_call | solution.py:294
  71.5 1.6 %collective-permute-start.15 = (bf16[1,528,128]{2,1,0:T(8,128)(2,1)S(1)}, bf16[1,528,128]{2,1,0:T(8,128)(2,1)S(1)}, u32[]{:S(2)}, u32[]{:S(2)}) collective-permute-start(bf16[1,528,128]{2,1,0:T(8,128)(2,1)S(1)} %shard_map.92), channel_id=1, source_target_pairs={{0,2},{2,0},{4,6},{6,4},{8,10},{10,8},{12,14},{14,12},{1,3},{3,1},... | collective-permute-start | bytes 405512 | tf_op jit(solution)/shard_map/ppermute | solution.py:435
  73.1 2.9 %shard_map.95 = bf16[2,528,128]{2,1,0:T(8,128)(2,1)S(1)} custom-call(bf16[512,256]{1,0:T(8,128)(2,1)S(1)} %collective-permute-done.18.refs_0_, s32[8,128]{1,0:T(8,128)S(1)} %bitcast.10, s32[8,128]{1,0:T(8,128)S(1)} %bitcast.19, bf16[2,2048,256]{2,1,0:T(8,128)(2,1)S(1)} %get-tuple-element.27.refs_3_, bf16[2,2048,256]{2,1,0:T(8,128)(2,1)S(1)} %get-tuple-element.28.refs_4_), custom_call_target="tpu_custom_call" | custom-call | flops 2147483648 | bytes 2621440 | tf_op jit(solution)/shard_map/pallas_call | solution.py:294
  76.5 3.4 %shard_map.85.refs_0_ = f32[2,520,128]{2,1,0:T(8,128)S(1)} custom-call(bf16[512,256]{1,0:T(8,128)(2,1)S(1)} %reshape.16.refs_0_, s32[8,128]{1,0:T(8,128)S(1)} %bitcast.11, s32[8,128]{1,0:T(8,128)S(1)} %bitcast.20, bf16[2,2048,256]{2,1,0:T(8,128)(2,1)S(1)} %get-tuple-element.23.refs_3_.refs_4_, bf16[2,2048,256]{2,1,0:T(8,128)(2,1)S(1)} %get-tuple-element.24.refs_4_.refs_5_), custom_call_target="tpu_custom_call" | custom-call | flops 2147483648 | bytes 2621440 | tf_op jit(solution)/shard_map/pallas_call | solution.py:294
  81.8 1.7 %collective-permute-start.12 = (bf16[2,528,128]{2,1,0:T(8,128)(2,1)S(1)}, bf16[2,528,128]{2,1,0:T(8,128)(2,1)S(1)}, u32[]{:S(2)}, u32[]{:S(2)}) collective-permute-start(bf16[2,528,128]{2,1,0:T(8,128)(2,1)S(1)} %shard_map.89), channel_id=1, source_target_pairs={{0,8},{2,10},{4,12},{6,14},{8,0},{10,2},{12,4},{14,6},{1,9},{3,11}... | collective-permute-start | bytes 811016 | tf_op jit(solution)/shard_map/ppermute | solution.py:435
  83.5 1.5 %shard_map.90.own_ref = f32[1,520,128]{2,1,0:T(8,128)S(1)} custom-call(bf16[512,256]{1,0:T(8,128)(2,1)S(1)} %collective-permute-done.5.refs_0_, s32[8,128]{1,0:T(8,128)S(1)} %bitcast.13, s32[8,128]{1,0:T(8,128)S(1)} %bitcast.22, bf16[2,2048,256]{2,1,0:T(8,128)(2,1)S(1)} %get-tuple-element.27.refs_3_, bf16[2,2048,256]{2,1,0:T(8,128)(2,1)S(1)} %get-tuple-element.28.refs_4_), custom_call_target="tpu_custom_call" | custom-call | flops 1073741824 | bytes 1310720 | tf_op jit(solution)/shard_map/pallas_call | solution.py:294
  86.9 1.7 %collective-permute-start.16 = (bf16[1,528,128]{2,1,0:T(8,128)(2,1)S(1)}, bf16[1,528,128]{2,1,0:T(8,128)(2,1)S(1)}, u32[]{:S(2)}, u32[]{:S(2)}) collective-permute-start(bf16[1,528,128]{2,1,0:T(8,128)(2,1)S(1)} %shard_map.94), channel_id=1, source_target_pairs={{0,8},{2,10},{4,12},{6,14},{8,0},{10,2},{12,4},{14,6},{1,9},{3,11}... | collective-permute-start | bytes 405512 | tf_op jit(solution)/shard_map/ppermute | solution.py:435
  88.6 2.8 %shard_map.87.refs_1_ = f32[2,520,128]{2,1,0:T(8,128)S(1)} custom-call(bf16[512,256]{1,0:T(8,128)(2,1)S(1)} %reshape.17.refs_0_, s32[8,128]{1,0:T(8,128)S(1)} %bitcast.14, s32[8,128]{1,0:T(8,128)S(1)} %bitcast.23, bf16[2,2048,256]{2,1,0:T(8,128)(2,1)S(1)} %get-tuple-element.27.refs_3_, bf16[2,2048,256]{2,1,0:T(8,128)(2,1)S(1)} %get-tuple-element.28.refs_4_), custom_call_target="tpu_custom_call" | custom-call | flops 2147483648 | bytes 2621440 | tf_op jit(solution)/shard_map/pallas_call | solution.py:294
  91.3 14.4 %collective-permute-done.14.refs_3_ = bf16[1,528,128]{2,1,0:T(8,128)(2,1)S(1)} collective-permute-done((bf16[1,528,128]{2,1,0:T(8,128)(2,1)S(1)}, bf16[1,528,128]{2,1,0:T(8,128)(2,1)S(1)}, u32[]{:S(2)}, u32[]{:S(2)}) %collective-permute-start.14) | collective-permute-done | bytes 135200 | tf_op jit(solution)/shard_map/ppermute | solution.py:435
  105.7 1.8 %collective-permute-done.16.refs_4_ = bf16[1,528,128]{2,1,0:T(8,128)(2,1)S(1)} collective-permute-done((bf16[1,528,128]{2,1,0:T(8,128)(2,1)S(1)}, bf16[1,528,128]{2,1,0:T(8,128)(2,1)S(1)}, u32[]{:S(2)}, u32[]{:S(2)}) %collective-permute-start.16) | collective-permute-done | bytes 135200 | tf_op jit(solution)/shard_map/ppermute | solution.py:435
  (55 shorter events, 12.2 us)
Async XLA Ops:
  0.7 13.3 %copy-start.6 = (bf16[128,4,512]{2,1,0:T(4,128)(2,1)S(1)}, bf16[128,4,512]{2,1,0:T(4,128)(2,1)}, u32[]{:S(2)}) copy-start(bf16[128,4,512]{2,1,0:T(4,128)(2,1)} %param.12) | copy-start | bytes 1572868
  10.9 17.6 %collective-permute-start.3 = (bf16[2,512,256]{2,1,0:T(8,128)(2,1)S(1)}, bf16[2,512,256]{2,1,0:T(8,128)(2,1)S(1)}, u32[]{:S(2)}, u32[]{:S(2)}) collective-permute-start(bf16[2,512,256]{2,1,0:T(8,128)(2,1)S(1)} %get-tuple-element.20.refs_3_), channel_id=1, source_target_pairs={{0,2},{2,0},{4,6},{6,4},{8,10},{10,8},{12,14},{14,12},{1,3},{3,1},... | collective-permute-start | bytes 1572872 | tf_op jit(solution)/shard_map/ppermute | solution.py:435
  14.3 15.2 %collective-permute-start = (bf16[512,256]{1,0:T(8,128)(2,1)S(1)}, bf16[512,256]{1,0:T(8,128)(2,1)S(1)}, u32[]{:S(2)}, u32[]{:S(2)}) collective-permute-start(bf16[512,256]{1,0:T(8,128)(2,1)S(1)} %reshape.16.refs_0_), channel_id=1, source_target_pairs={{0,8},{2,10},{4,12},{6,14},{8,0},{10,2},{12,4},{14,6},{1,9},{3,11}... | collective-permute-start | bytes 786440 | tf_op jit(solution)/shard_map/ppermute | solution.py:435
  20.3 9.0 %copy-start.7 = (s32[32]{0:T(128)S(1)}, s32[32]{0:T(128)}, u32[]{:S(2)}) copy-start(s32[32]{0:T(128)} %param.13) | copy-start | bytes 388
  20.3 34.9 %copy-start.2 = (s32[1024]{0:T(1024)S(1)}, s32[1024]{0:T(1024)}, u32[]{:S(2)}) copy-start(s32[1024]{0:T(1024)} %param.14) | copy-start | bytes 12292
  20.3 34.9 %copy-start.3 = (s32[1024]{0:T(1024)S(1)}, s32[1024]{0:T(1024)}, u32[]{:S(2)}) copy-start(s32[1024]{0:T(1024)} %param.15) | copy-start | bytes 12292
  26.8 26.6 %collective-permute-start.8 = (bf16[2,512,256]{2,1,0:T(8,128)(2,1)S(1)}, bf16[2,512,256]{2,1,0:T(8,128)(2,1)S(1)}, u32[]{:S(2)}, u32[]{:S(2)}) collective-permute-start(bf16[2,512,256]{2,1,0:T(8,128)(2,1)S(1)} %shard_map.83.refs_3_), channel_id=1, source_target_pairs={{0,4},{2,6},{4,0},{6,2},{8,12},{10,14},{12,8},{14,10},{1,5},{3,7},... | collective-permute-start | bytes 1572872 | tf_op jit(solution)/shard_map/ppermute | solution.py:435
  28.5 25.0 %collective-permute-start.2 = (bf16[2,512,256]{2,1,0:T(8,128)(2,1)S(1)}, bf16[2,512,256]{2,1,0:T(8,128)(2,1)S(1)}, u32[]{:S(2)}, u32[]{:S(2)}) collective-permute-start(bf16[2,512,256]{2,1,0:T(8,128)(2,1)S(1)} %get-tuple-element.20.refs_3_), channel_id=1, source_target_pairs={{0,16},{16,0},{1,17},{17,1},{2,18},{18,2},{3,19},{19,3},{4,20},{20... | collective-permute-start | bytes 1572872 | tf_op jit(solution)/shard_map/ppermute | solution.py:438
  28.5 26.6 %collective-permute-start.4 = (bf16[2,512,256]{2,1,0:T(8,128)(2,1)S(1)}, bf16[2,512,256]{2,1,0:T(8,128)(2,1)S(1)}, u32[]{:S(2)}, u32[]{:S(2)}) collective-permute-start(bf16[2,512,256]{2,1,0:T(8,128)(2,1)S(1)} %collective-permute-done.3.refs_5_), channel_id=1, source_target_pairs={{0,16},{16,0},{1,17},{17,1},{2,18},{18,2},{3,19},{19,3},{4,20},{20... | collective-permute-start | bytes 1572872 | tf_op jit(solution)/shard_map/ppermute | solution.py:438
  29.0 17.4 %collective-permute-start.5 = (bf16[512,256]{1,0:T(8,128)(2,1)S(1)}, bf16[512,256]{1,0:T(8,128)(2,1)S(1)}, u32[]{:S(2)}, u32[]{:S(2)}) collective-permute-start(bf16[512,256]{1,0:T(8,128)(2,1)S(1)} %reshape.17.refs_0_), channel_id=1, source_target_pairs={{0,8},{2,10},{4,12},{6,14},{8,0},{10,2},{12,4},{14,6},{1,9},{3,11}... | collective-permute-start | bytes 786440 | tf_op jit(solution)/shard_map/ppermute | solution.py:435
  29.4 23.5 %collective-permute-start.1 = (bf16[512,256]{1,0:T(8,128)(2,1)S(1)}, bf16[512,256]{1,0:T(8,128)(2,1)S(1)}, u32[]{:S(2)}, u32[]{:S(2)}) collective-permute-start(bf16[512,256]{1,0:T(8,128)(2,1)S(1)} %collective-permute-done.refs_0_), channel_id=1, source_target_pairs={{0,4},{2,6},{4,0},{6,2},{8,12},{10,14},{12,8},{14,10},{1,5},{3,7},... | collective-permute-start | bytes 786440 | tf_op jit(solution)/shard_map/ppermute | solution.py:435
  46.4 12.3 %collective-permute-start.11 = (bf16[512,256]{1,0:T(8,128)(2,1)S(1)}, bf16[512,256]{1,0:T(8,128)(2,1)S(1)}, u32[]{:S(2)}, u32[]{:S(2)}) collective-permute-start(bf16[512,256]{1,0:T(8,128)(2,1)S(1)} %reshape.16.refs_0_), channel_id=1, source_target_pairs={{0,4},{2,6},{4,0},{6,2},{8,12},{10,14},{12,8},{14,10},{1,5},{3,7},... | collective-permute-start | bytes 786440 | tf_op jit(solution)/shard_map/ppermute | solution.py:435
  52.9 20.2 %collective-permute-start.18 = (bf16[512,256]{1,0:T(8,128)(2,1)S(1)}, bf16[512,256]{1,0:T(8,128)(2,1)S(1)}, u32[]{:S(2)}, u32[]{:S(2)}) collective-permute-start(bf16[512,256]{1,0:T(8,128)(2,1)S(1)} %reshape.17.refs_0_), channel_id=1, source_target_pairs={{0,2},{2,0},{4,6},{6,4},{8,10},{10,8},{12,14},{14,12},{1,3},{3,1},... | collective-permute-start | bytes 786440 | tf_op jit(solution)/shard_map/ppermute | solution.py:435
  53.5 13.9 %collective-permute-start.7 = (bf16[2,512,256]{2,1,0:T(8,128)(2,1)S(1)}, bf16[2,512,256]{2,1,0:T(8,128)(2,1)S(1)}, u32[]{:S(2)}, u32[]{:S(2)}) collective-permute-start(bf16[2,512,256]{2,1,0:T(8,128)(2,1)S(1)} %shard_map.83.refs_3_), channel_id=1, source_target_pairs={{0,16},{16,0},{1,17},{17,1},{2,18},{18,2},{3,19},{19,3},{4,20},{20... | collective-permute-start | bytes 1572872 | tf_op jit(solution)/shard_map/ppermute | solution.py:438
  53.5 13.5 %collective-permute-start.6 = (bf16[512,256]{1,0:T(8,128)(2,1)S(1)}, bf16[512,256]{1,0:T(8,128)(2,1)S(1)}, u32[]{:S(2)}, u32[]{:S(2)}) collective-permute-start(bf16[512,256]{1,0:T(8,128)(2,1)S(1)} %collective-permute-done.5.refs_0_), channel_id=1, source_target_pairs={{0,2},{2,0},{4,6},{6,4},{8,10},{10,8},{12,14},{14,12},{1,3},{3,1},... | collective-permute-start | bytes 786440 | tf_op jit(solution)/shard_map/ppermute | solution.py:435
  55.0 12.3 %collective-permute-start.9 = (bf16[2,512,256]{2,1,0:T(8,128)(2,1)S(1)}, bf16[2,512,256]{2,1,0:T(8,128)(2,1)S(1)}, u32[]{:S(2)}, u32[]{:S(2)}) collective-permute-start(bf16[2,512,256]{2,1,0:T(8,128)(2,1)S(1)} %collective-permute-done.8.refs_5_), channel_id=1, source_target_pairs={{0,16},{16,0},{1,17},{17,1},{2,18},{18,2},{3,19},{19,3},{4,20},{20... | collective-permute-start | bytes 1572872 | tf_op jit(solution)/shard_map/ppermute | solution.py:438
  65.3 42.9 %collective-permute-start.17 = (bf16[2,528,128]{2,1,0:T(8,128)(2,1)S(1)}, bf16[2,528,128]{2,1,0:T(8,128)(2,1)S(1)}, u32[]{:S(2)}, u32[]{:S(2)}) collective-permute-start(bf16[2,528,128]{2,1,0:T(8,128)(2,1)S(1)} %get-tuple-element.32), channel_id=1, source_target_pairs={{0,4},{2,6},{4,0},{6,2},{8,12},{10,14},{12,8},{14,10},{1,5},{3,7},... | collective-permute-start | bytes 811016 | tf_op jit(solution)/shard_map/ppermute | solution.py:435
  66.9 14.5 %collective-permute-start.10 = (bf16[2,528,128]{2,1,0:T(8,128)(2,1)S(1)}, bf16[2,528,128]{2,1,0:T(8,128)(2,1)S(1)}, u32[]{:S(2)}, u32[]{:S(2)}) collective-permute-start(bf16[2,528,128]{2,1,0:T(8,128)(2,1)S(1)} %get-tuple-element.29), channel_id=1, source_target_pairs={{0,4},{2,6},{4,0},{6,2},{8,12},{10,14},{12,8},{14,10},{1,5},{3,7},... | collective-permute-start | bytes 811016 | tf_op jit(solution)/shard_map/ppermute | solution.py:435
  69.4 15.6 %collective-permute-start.13 = (bf16[1,528,128]{2,1,0:T(8,128)(2,1)S(1)}, bf16[1,528,128]{2,1,0:T(8,128)(2,1)S(1)}, u32[]{:S(2)}, u32[]{:S(2)}) collective-permute-start(bf16[1,528,128]{2,1,0:T(8,128)(2,1)S(1)} %get-tuple-element.31), channel_id=1, source_target_pairs={{0,2},{2,0},{4,6},{6,4},{8,10},{10,8},{12,14},{14,12},{1,3},{3,1},... | collective-permute-start | bytes 405512 | tf_op jit(solution)/shard_map/ppermute | solution.py:435
  71.5 15.1 %collective-permute-start.15 = (bf16[1,528,128]{2,1,0:T(8,128)(2,1)S(1)}, bf16[1,528,128]{2,1,0:T(8,128)(2,1)S(1)}, u32[]{:S(2)}, u32[]{:S(2)}) collective-permute-start(bf16[1,528,128]{2,1,0:T(8,128)(2,1)S(1)} %shard_map.92), channel_id=1, source_target_pairs={{0,2},{2,0},{4,6},{6,4},{8,10},{10,8},{12,14},{14,12},{1,3},{3,1},... | collective-permute-start | bytes 405512 | tf_op jit(solution)/shard_map/ppermute | solution.py:435
  76.0 32.2 %collective-permute-start.19 = (bf16[2,528,128]{2,1,0:T(8,128)(2,1)S(1)}, bf16[2,528,128]{2,1,0:T(8,128)(2,1)S(1)}, u32[]{:S(2)}, u32[]{:S(2)}) collective-permute-start(bf16[2,528,128]{2,1,0:T(8,128)(2,1)S(1)} %shard_map.95), channel_id=1, source_target_pairs={{0,2},{2,0},{4,6},{6,4},{8,10},{10,8},{12,14},{14,12},{1,3},{3,1},... | collective-permute-start | bytes 811016 | tf_op jit(solution)/shard_map/ppermute | solution.py:435
  81.8 25.7 %collective-permute-start.12 = (bf16[2,528,128]{2,1,0:T(8,128)(2,1)S(1)}, bf16[2,528,128]{2,1,0:T(8,128)(2,1)S(1)}, u32[]{:S(2)}, u32[]{:S(2)}) collective-permute-start(bf16[2,528,128]{2,1,0:T(8,128)(2,1)S(1)} %shard_map.89), channel_id=1, source_target_pairs={{0,8},{2,10},{4,12},{6,14},{8,0},{10,2},{12,4},{14,6},{1,9},{3,11}... | collective-permute-start | bytes 811016 | tf_op jit(solution)/shard_map/ppermute | solution.py:435
  85.3 20.5 %collective-permute-start.14 = (bf16[1,528,128]{2,1,0:T(8,128)(2,1)S(1)}, bf16[1,528,128]{2,1,0:T(8,128)(2,1)S(1)}, u32[]{:S(2)}, u32[]{:S(2)}) collective-permute-start(bf16[1,528,128]{2,1,0:T(8,128)(2,1)S(1)} %shard_map.91), channel_id=1, source_target_pairs={{0,8},{2,10},{4,12},{6,14},{8,0},{10,2},{12,4},{14,6},{1,9},{3,11}... | collective-permute-start | bytes 405512 | tf_op jit(solution)/shard_map/ppermute | solution.py:435
  86.9 20.6 %collective-permute-start.16 = (bf16[1,528,128]{2,1,0:T(8,128)(2,1)S(1)}, bf16[1,528,128]{2,1,0:T(8,128)(2,1)S(1)}, u32[]{:S(2)}, u32[]{:S(2)}) collective-permute-start(bf16[1,528,128]{2,1,0:T(8,128)(2,1)S(1)} %shard_map.94), channel_id=1, source_target_pairs={{0,8},{2,10},{4,12},{6,14},{8,0},{10,2},{12,4},{14,6},{1,9},{3,11}... | collective-permute-start | bytes 405512 | tf_op jit(solution)/shard_map/ppermute | solution.py:435
  (4 other events, 13.3 us)
